TPU v7x, 512 devices: a whole 4x8x8 slice. The times are simulated.
512 devices in a mesh: ctx: 16 (over z, core), tis: 8 (over y), rep: 4 (over x).
Axes of the slice: x: 4, y: 8, z: 8, core: 2. Of those that a mesh axis runs over, the one named last changes fastest.
Arguments:
- donor_feat: bfloat16 [4, 256, 256], P('rep', 'ctx'), may hold values from -6 to 6
- acceptor_feat: bfloat16 [4, 256, 256], P('rep', 'ctx'), may hold values from -6 to 6
- donor_pos: int32 [4, 256], P('rep', 'ctx'), may hold values from 0 to 65535
- acceptor_pos: int32 [4, 256], P('rep'), may hold values from 0 to 65535
- pair_mask: int32 [4, 256, 80], P('rep', 'ctx'), may hold values from 0 to 1
- targets: int32 [4, 256, 32], P('rep', 'ctx', 'tis'), may hold values from 0 to 80, as said below
- dist_table: bfloat16 [128, 256], replicated, may hold values from -3 to 3
- hidden_weights: bfloat16 [32, 256, 512], P('tis'), may hold values from -0.375 to 0.375
- output_weights: bfloat16 [32, 512], P('tis')
Outputs:
- donor_loss: float32 [4, 256, 32], P('rep', 'ctx', 'tis')
- grad_hidden: float32 [32, 256, 512], P('tis', ('ctx', 'rep'))
- grad_acceptor: float32 [4, 256, 256], P('rep', 'ctx')
Inputs may be any that keep to these rules, and one draw needn't show every extreme that they name: `targets`: each target is a valid slot of its donor, or 80 for no splice.
All inputs are finite; a program needn't handle non-finite values.
Results may differ from a plain program's by a relative error of at most 0.002.
The roundings to bfloat16 on the way count: a program that leaves them out, or rounds other values in their place, can miss the bound.
Values may be sent and summed in bfloat16 or wider, within the bound.
A program may use at most 64 MiB of HBM per device.

v0:
```python
import jax
import jax.numpy as jnp
from jax import lax
from jax.sharding import PartitionSpec as P

BLOCK_BP = 65536
SPAN_BLOCKS = 4
BIN_BP = 2048
BINS = 128


def passed_along(value, axis, steps):
    count = lax.axis_size(axis)
    first, last = (max(0, -steps), min(count, count - steps))
    return lax.ppermute(value, axis, [(source, source + steps) for source in range(first, last)])


def silu_grad(values):
    sig = jax.nn.sigmoid(values)
    return sig * (1.0 + values * (1.0 - sig))


def on_device(
    donor_feat,
    acceptor_feat,
    donor_pos,
    acceptor_pos,
    pair_mask,
    targets,
    dist_table,
    hidden_weights,
    output_weights,
):
    seq_dev, don_blk, width = donor_feat.shape
    acc_blk = acceptor_feat.shape[1]
    blocks = lax.axis_size("ctx")
    reach = SPAN_BLOCKS + 1
    slots = reach * acc_blk
    here = lax.axis_index("ctx")
    pieces = [acceptor_feat]
    current = acceptor_feat
    for offset in range(1, reach):
        current = passed_along(current, "ctx", -1)
        pieces.append(current)
    window = jnp.stack(pieces, axis=1).reshape(seq_dev, slots, width)
    pos_pad = jnp.concatenate(
        [acceptor_pos, jnp.zeros((seq_dev, SPAN_BLOCKS * acc_blk), jnp.int32)], axis=1
    )
    pos_win = lax.dynamic_slice_in_dim(pos_pad, here * acc_blk, slots, 1)
    slot_block = jnp.arange(slots, dtype=jnp.int32) // acc_blk
    inchain = here + slot_block < blocks
    dist = slot_block * BLOCK_BP + pos_win[:, None, :] - donor_pos[:, :, None]
    valid = (pair_mask > 0) & (dist > 0) & (dist <= SPAN_BLOCKS * BLOCK_BP) & inchain[None, None, :]
    bins = jnp.clip((dist - 1) // BIN_BP, 0, BINS - 1)
    lookup = (
        (bins[..., None] == jnp.arange(BINS, dtype=jnp.int32))
        .astype(jnp.bfloat16)
        .reshape(-1, BINS)
    )
    table = jnp.dot(lookup, dist_table, preferred_element_type=jnp.float32).reshape(
        seq_dev, don_blk, slots, width
    )
    pre = (
        donor_feat.astype(jnp.float32)[:, :, None, :] + window.astype(jnp.float32)[:, None] + table
    )
    flat = jax.nn.silu(pre).astype(jnp.bfloat16).reshape(-1, width)
    grad_pair = jnp.zeros((flat.shape[0], width), jnp.float32)
    losses = []
    fulls = []
    slot_ids = jnp.arange(slots, dtype=jnp.int32)
    for tissue in range(hidden_weights.shape[0]):
        w_in = hidden_weights[tissue]
        w_out = output_weights[tissue]
        goal = targets[:, :, tissue]
        hid = jnp.dot(flat, w_in, preferred_element_type=jnp.float32)
        act = jax.nn.silu(hid).astype(jnp.bfloat16)
        logits = jnp.dot(act, w_out, preferred_element_type=jnp.float32).reshape(
            seq_dev, don_blk, slots
        )
        masked = jnp.where(valid, logits, -jnp.inf)
        top = jnp.maximum(jnp.max(masked, axis=-1), 0.0)
        expo = jnp.exp(masked - top[..., None])
        total = jnp.sum(expo, axis=-1) + jnp.exp(-top)
        picked = jnp.take_along_axis(logits, jnp.minimum(goal, slots - 1)[..., None], axis=-1)[
            ..., 0
        ]
        picked = jnp.where(goal == slots, 0.0, picked)
        losses.append(top + jnp.log(total) - picked)
        onehot = (goal[..., None] == slot_ids).astype(jnp.float32)
        grad_logits = expo / total[..., None] - onehot
        grad_act = grad_logits.reshape(-1)[:, None] * w_out.astype(jnp.float32)[None, :]
        grad_hid = (grad_act * silu_grad(hid)).astype(jnp.bfloat16)
        grad_pair = grad_pair + lax.dot_general(
            grad_hid, w_in, (((1,), (1,)), ((), ())), preferred_element_type=jnp.float32
        )
        fulls.append(
            lax.dot_general(
                flat, grad_hid, (((0,), (0,)), ((), ())), preferred_element_type=jnp.float32
            )
        )
    stacked = jnp.stack(fulls, axis=1)
    grad_hidden = jnp.transpose(
        lax.psum_scatter(stacked, ("ctx", "rep"), scatter_dimension=0, tiled=True), (1, 0, 2)
    )
    grad_pre = grad_pair.reshape(seq_dev, don_blk, slots, width) * silu_grad(pre)
    contrib = jnp.sum(grad_pre, axis=1).reshape(seq_dev, reach, acc_blk, width)
    carried = contrib[:, reach - 1]
    for offset in range(reach - 2, -1, -1):
        carried = passed_along(carried, "ctx", 1) + contrib[:, offset]
    grad_acceptor = lax.psum(carried, "tis")
    donor_loss = jnp.stack(losses, axis=-1)
    return (donor_loss, grad_hidden, grad_acceptor)


def solution(mesh):
    placed = (
        P("rep", "ctx", None),
        P("rep", "ctx", None),
        P("rep", "ctx"),
        P("rep", None),
        P("rep", "ctx", None),
        P("rep", "ctx", "tis"),
        P(),
        P("tis", None, None),
        P("tis", None),
    )
    return jax.shard_map(
        on_device,
        mesh=mesh,
        in_specs=placed,
        out_specs=(P("rep", "ctx", "tis"), P("tis", ("ctx", "rep"), None), P("rep", "ctx", None)),
        check_vma=False,
    )
```

profile of v0, /device:TPU:1, one launch (start us, length us, event | category | flops | bytes accessed | tf_op | source)
XLA Modules:
  0.0 280.2 jit_solution(4810384354852864490)
XLA Ops:
  7.2 8.8 %collective-permute-start = (bf16[1,16,256]{2,1,0:T(8,128)(2,1)}, bf16[1,16,256]{2,1,0:T(8,128)(2,1)S(1)}, u32[]{:S(2)}, u32[]{:S(2)}) collective-permute-start(bf16[1,16,256]{2,1,0:T(8,128)(2,1)} %param.12), channel_id=1, source_target_pairs={{32,0},{64,32},{96,64},{128,96},{160,128},{192,160},{224,192},{256... | collective-permute-start | bytes 24584 | tf_op jit(solution)/shard_map/ppermute | solution.py:15
  20.7 1.9 collective-permute-start.1
  22.7 3.0 %collective-permute-done.1 = bf16[1,16,256]{2,1,0:T(8,128)(2,1)S(1)} collective-permute-done((bf16[1,16,256]{2,1,0:T(8,128)(2,1)S(1)}, bf16[1,16,256]{2,1,0:T(8,128)(2,1)S(1)}, u32[]{:S(2)}, u32[]{:S(2)}) %collective-permute-start.1) | collective-permute-done | bytes 8224 | tf_op jit(solution)/shard_map/ppermute | solution.py:15
  25.7 1.9 collective-permute-start.2
  27.6 3.0 %collective-permute-done.2 = bf16[1,16,256]{2,1,0:T(8,128)(2,1)S(1)} collective-permute-done((bf16[1,16,256]{2,1,0:T(8,128)(2,1)S(1)}, bf16[1,16,256]{2,1,0:T(8,128)(2,1)S(1)}, u32[]{:S(2)}, u32[]{:S(2)}) %collective-permute-start.2) | collective-permute-done | bytes 8224 | tf_op jit(solution)/shard_map/ppermute | solution.py:15
  30.7 1.9 collective-permute-start.3
  32.6 3.0 %collective-permute-done.3 = bf16[1,16,256]{2,1,0:T(8,128)(2,1)S(1)} collective-permute-done((bf16[1,16,256]{2,1,0:T(8,128)(2,1)S(1)}, bf16[1,16,256]{2,1,0:T(8,128)(2,1)S(1)}, u32[]{:S(2)}, u32[]{:S(2)}) %collective-permute-start.3) | collective-permute-done | bytes 8224 | tf_op jit(solution)/shard_map/ppermute | solution.py:15
  35.7 1.7 multiply_convert_fusion.8
  38.2 2.3 multiply_convert_fusion.4
  40.5 2.3 multiply_convert_fusion.5
  42.8 2.3 multiply_convert_fusion.6
  49.0 1.4 convolution_bitcast_fusion.3
  50.4 2.5 fusion.10
  53.0 2.7 multiply_convert_fusion
  57.1 2.7 multiply_convert_fusion.1
  61.3 2.7 multiply_convert_fusion.2
  68.7 1.9 collective-permute-start.4
  70.6 1.5 pad_maximum_fusion
  72.2 3.5 %collective-permute-start.5 = (f32[1,16,256]{2,1,0:T(8,128)S(1)}, f32[1,16,256]{2,1,0:T(8,128)S(1)}, u32[]{:S(2)}, u32[]{:S(2)}) collective-permute-start(f32[1,16,256]{2,1,0:T(8,128)S(1)} %fusion.26), channel_id=1, source_target_pairs={{0,32},{32,64},{64,96},{96,128},{128,160},{160,192},{192,224},{224... | collective-permute-start | bytes 49160 | tf_op jit(solution)/shard_map/ppermute | solution.py:15
  80.3 1.9 collective-permute-start.6
  83.3 3.9 %collective-permute-start.7 = (f32[1,16,256]{2,1,0:T(8,128)S(1)}, f32[1,16,256]{2,1,0:T(8,128)S(1)}, u32[]{:S(2)}, u32[]{:S(2)}) collective-permute-start(f32[1,16,256]{2,1,0:T(8,128)S(1)} %fusion.24), channel_id=1, source_target_pairs={{0,32},{32,64},{64,96},{96,128},{128,160},{160,192},{192,224},{224... | collective-permute-start | bytes 49160 | tf_op jit(solution)/shard_map/ppermute | solution.py:15
  88.1 22.4 %psum.7 = f32[1,16,256]{2,1,0:T(8,128)} all-reduce(f32[1,16,256]{2,1,0:T(8,128)S(1)} %fusion.23), channel_id=1, replica_groups=mesh['ctx'=16,'tis'=8,'rep'=4] {'tis'}, use_global_device_ids=true, to_apply=%region_10.12 | all-reduce | flops 4096 | bytes 32768 | tf_op jit(solution)/shard_map/psum | solution.py:110
  110.5 161.4 %all-reduce.4.cloned.1.call-done = f32[256,4,512]{2,0,1:T(8,128)} async-done(((f32[256,4,512]{2,0,1:T(8,128)}), f32[256,4,512]{2,0,1:T(8,128)}) %all-reduce.4.cloned.1.call-update) | async-done | bytes 2097168
  271.9 1.5 dynamic-slice_bitcast_fusion
  (89 shorter events, 22.8 us)
Async XLA Ops:
  7.2 28.5 %copy-start = (bf16[128,256]{1,0:T(8,128)(2,1)S(1)}, bf16[128,256]{1,0:T(8,128)(2,1)}, u32[]{:S(2)}) copy-start(bf16[128,256]{1,0:T(8,128)(2,1)} %param.17) | copy-start | bytes 196612
  7.2 264.7 %all-reduce.4.cloned.1.call-start = ((), (), s32[]{:S(2)}) async-start(), calls=%async_computation | async-start | bytes 4194304
  7.2 13.5 %collective-permute-start = (bf16[1,16,256]{2,1,0:T(8,128)(2,1)}, bf16[1,16,256]{2,1,0:T(8,128)(2,1)S(1)}, u32[]{:S(2)}, u32[]{:S(2)}) collective-permute-start(bf16[1,16,256]{2,1,0:T(8,128)(2,1)} %param.12), channel_id=1, source_target_pairs={{32,0},{64,32},{96,64},{128,96},{160,128},{192,160},{224,192},{256... | collective-permute-start | bytes 24584 | tf_op jit(solution)/shard_map/ppermute | solution.py:15
  20.7 5.0 %collective-permute-start.1 = (bf16[1,16,256]{2,1,0:T(8,128)(2,1)S(1)}, bf16[1,16,256]{2,1,0:T(8,128)(2,1)S(1)}, u32[]{:S(2)}, u32[]{:S(2)}) collective-permute-start(bf16[1,16,256]{2,1,0:T(8,128)(2,1)S(1)} %collective-permute-done), channel_id=1, source_target_pairs={{32,0},{64,32},{96,64},{128,96},{160,128},{192,160},{224,192},{256... | collective-permute-start | bytes 24584 | tf_op jit(solution)/shard_map/ppermute | solution.py:15
  25.7 5.0 %collective-permute-start.2 = (bf16[1,16,256]{2,1,0:T(8,128)(2,1)S(1)}, bf16[1,16,256]{2,1,0:T(8,128)(2,1)S(1)}, u32[]{:S(2)}, u32[]{:S(2)}) collective-permute-start(bf16[1,16,256]{2,1,0:T(8,128)(2,1)S(1)} %collective-permute-done.1), channel_id=1, source_target_pairs={{32,0},{64,32},{96,64},{128,96},{160,128},{192,160},{224,192},{256... | collective-permute-start | bytes 24584 | tf_op jit(solution)/shard_map/ppermute | solution.py:15
  30.7 5.0 %collective-permute-start.3 = (bf16[1,16,256]{2,1,0:T(8,128)(2,1)S(1)}, bf16[1,16,256]{2,1,0:T(8,128)(2,1)S(1)}, u32[]{:S(2)}, u32[]{:S(2)}) collective-permute-start(bf16[1,16,256]{2,1,0:T(8,128)(2,1)S(1)} %collective-permute-done.2), channel_id=1, source_target_pairs={{32,0},{64,32},{96,64},{128,96},{160,128},{192,160},{224,192},{256... | collective-permute-start | bytes 24584 | tf_op jit(solution)/shard_map/ppermute | solution.py:15
  35.7 1.7 copy-start.6
  42.8 2.3 copy-start.8
  45.7 1.7 copy-start.10
  45.7 1.7 copy-start.11
  64.0 1.3 copy-start.1
  64.0 1.6 copy-start.7
  66.8 1.3 copy-start.5
  67.4 3.2 %copy-start.2 = (f32[256,1,512]{2,0,1:T(8,128)S(1)}, f32[256,1,512]{2,0,1:T(8,128)}, u32[]{:S(2)}) copy-start(f32[256,1,512]{2,0,1:T(8,128)} %convolution_bitcast_fusion.3) | copy-start | bytes 1572868
  67.4 3.2 %copy-start.3 = (f32[256,1,512]{2,0,1:T(8,128)S(1)}, f32[256,1,512]{2,0,1:T(8,128)}, u32[]{:S(2)}) copy-start(f32[256,1,512]{2,0,1:T(8,128)} %convolution_bitcast_fusion) | copy-start | bytes 1572868
  67.4 3.2 %copy-start.4 = (f32[256,1,512]{2,0,1:T(8,128)S(1)}, f32[256,1,512]{2,0,1:T(8,128)}, u32[]{:S(2)}) copy-start(f32[256,1,512]{2,0,1:T(8,128)} %convolution_bitcast_fusion.1) | copy-start | bytes 1572868
  68.7 3.5 %collective-permute-start.4 = (f32[1,16,256]{2,1,0:T(8,128)S(1)}, f32[1,16,256]{2,1,0:T(8,128)S(1)}, u32[]{:S(2)}, u32[]{:S(2)}) collective-permute-start(f32[1,16,256]{2,1,0:T(8,128)S(1)} %slice_bitcast_fusion.4), channel_id=1, source_target_pairs={{0,32},{32,64},{64,96},{96,128},{128,160},{160,192},{192,224},{224... | collective-permute-start | bytes 49160 | tf_op jit(solution)/shard_map/ppermute | solution.py:15
  72.1 10.1 %copy-start.9 = (s32[1,16,4]{1,2,0:T(4,128)S(1)}, s32[1,16,4]{1,2,0:T(4,128)}, u32[]{:S(2)}) copy-start(s32[1,16,4]{1,2,0:T(4,128)} %param.16) | copy-start | bytes 772
  72.2 8.1 %collective-permute-start.5 = (f32[1,16,256]{2,1,0:T(8,128)S(1)}, f32[1,16,256]{2,1,0:T(8,128)S(1)}, u32[]{:S(2)}, u32[]{:S(2)}) collective-permute-start(f32[1,16,256]{2,1,0:T(8,128)S(1)} %fusion.26), channel_id=1, source_target_pairs={{0,32},{32,64},{64,96},{96,128},{128,160},{160,192},{192,224},{224... | collective-permute-start | bytes 49160 | tf_op jit(solution)/shard_map/ppermute | solution.py:15
  80.3 3.1 %collective-permute-start.6 = (f32[1,16,256]{2,1,0:T(8,128)S(1)}, f32[1,16,256]{2,1,0:T(8,128)S(1)}, u32[]{:S(2)}, u32[]{:S(2)}) collective-permute-start(f32[1,16,256]{2,1,0:T(8,128)S(1)} %fusion.25), channel_id=1, source_target_pairs={{0,32},{32,64},{64,96},{96,128},{128,160},{160,192},{192,224},{224... | collective-permute-start | bytes 49160 | tf_op jit(solution)/shard_map/ppermute | solution.py:15
  83.3 4.7 %collective-permute-start.7 = (f32[1,16,256]{2,1,0:T(8,128)S(1)}, f32[1,16,256]{2,1,0:T(8,128)S(1)}, u32[]{:S(2)}, u32[]{:S(2)}) collective-permute-start(f32[1,16,256]{2,1,0:T(8,128)S(1)} %fusion.24), channel_id=1, source_target_pairs={{0,32},{32,64},{64,96},{96,128},{128,160},{160,192},{192,224},{224... | collective-permute-start | bytes 49160 | tf_op jit(solution)/shard_map/ppermute | solution.py:15
Sparse Core Ops, SparseCore 0:
  72.2 199.5 all-reduce.3
where the time goes:
time: 282 us; the launch traced here: 280 us
  waiting for transfers between devices  172 us (61%)
  starting transfers between devices  25.8 us (9%)
  blocking collectives  22.4 us (8%)
  matrix products  20.5 us (7%)
  other arithmetic  15.4 us (5%)
  between operations  15.1 us (5%)
  local copies, waits for them, and re-layouts  9.11 us (3%)
    unnamed x2, waiting for transfers between devices  161 us
    ppermute x8, starting transfers between devices, passed_along(): lax.ppermute(value, axis, [(source, source + steps) for source in range(f...  25.8 us
    psum x1, blocking collectives, on_device(): grad_acceptor = lax.psum(carried, 'tis')  22.4 us
    ppermute x8, waiting for transfers between devices, passed_along(): lax.ppermute(value, axis, [(source, source + steps) for source in range(f...  10.5 us
    convert_element_type x4, other arithmetic, on_device(): grad_hid = (grad_act * silu_grad(hid)).astype(jnp.bfloat16)  9.15 us
    dot_general x4, matrix products, on_device(): hid = jnp.dot(flat, w_in, preferred_element_type=jnp.float32)  7.74 us
  transfers between devices with their start and end apart: 9, of which 6 were waited for; matrix products, arithmetic and copies ran while one was open for 4% of the time, Pallas kernels for 0%

commit v1 on v0

v1 whole, which is shorter than its diff:
```python
import functools

import jax
import jax.numpy as jnp
from jax import lax
from jax.experimental import pallas as pl
from jax.experimental.pallas import tpu as pltpu
from jax.sharding import PartitionSpec as P

MESH = pl.DeviceIdType.MESH
F32 = jnp.float32
BF16 = jnp.bfloat16
BLOCK_BP = 65536
SPAN = 4
REACH = SPAN + 1
BIN_BP = 2048
BINS = 128
BLK = 16
ROWS = BLK * BLK
SLOTS = REACH * BLK
WIDTH = 256
HIDDEN = 512
LANES = 128


def kernel(
    sizes,
    don_ref,
    acc_ref,
    dpos_ref,
    apos_ref,
    mask_ref,
    goal_ref,
    table_ref,
    w_ref,
    wo_ref,
    loss_ref,
    gw_ref,
    gacc_ref,
    window,
    mpad,
    perm,
    half_pair,
    pair_t,
    slope_pre,
    valid,
    slope,
    logit,
    grad_logit,
    grad_hid,
    out_cols,
    out_rows,
    goals,
    losses,
    part,
    from_core,
    by_rep,
    from_rep,
    by_z,
    from_z,
    contrib,
    from_ctx,
    by_tis,
    halo_send,
    halo_recv,
    core_send,
    core_recv,
    rep_send,
    rep_recv,
    z_send,
    z_recv,
    ctx_send,
    ctx_recv,
    tis_send,
    tis_recv,
):
    n_ctx, n_tis, n_rep, tissues = sizes
    n_z = n_ctx // 2
    ctx = lax.axis_index("ctx")
    tis = lax.axis_index("tis")
    rep = lax.axis_index("rep")
    core = lax.rem(ctx, 2)
    z = lax.div(ctx, 2)

    def at_ctx(offset):
        return {"ctx": lax.rem(ctx + (offset % n_ctx), n_ctx)}

    def at_tis(offset):
        return {"tis": lax.rem(tis + (offset % n_tis), n_tis)}

    def at_rep(offset):
        return {"rep": lax.rem(rep + (offset % n_rep), n_rep)}

    other_core = {"ctx": ctx + 1 - 2 * core}

    def remote(src, dst, send, recv, device):
        return pltpu.make_async_remote_copy(
            src_ref=src,
            dst_ref=dst,
            send_sem=send,
            recv_sem=recv,
            device_id=device,
            device_id_type=MESH,
        )

    def halo(k):
        return remote(
            acc_ref.at[0], window.at[k], halo_send.at[k - 1], halo_recv.at[k - 1], at_ctx(-k)
        )

    def to_core(t):
        return remote(
            part.at[t, 1 - core], from_core.at[t], core_send.at[t], core_recv.at[t], other_core
        )

    def to_rep(t, j):
        return remote(
            by_rep.at[t, lax.rem(rep + j, n_rep)],
            from_rep.at[t, j - 1],
            rep_send.at[t, j - 1],
            rep_recv.at[t, j - 1],
            at_rep(j),
        )

    def to_z(t, j):
        return remote(
            by_z.at[t, lax.rem(z + j, n_z)],
            from_z.at[t, j - 1],
            z_send.at[t, j - 1],
            z_recv.at[t, j - 1],
            at_ctx(2 * j),
        )

    def to_ctx(k):
        return remote(
            contrib.at[k], from_ctx.at[k - 1], ctx_send.at[k - 1], ctx_recv.at[k - 1], at_ctx(k)
        )

    def to_tis(j):
        return remote(
            by_tis.at[tis], by_tis.at[tis], tis_send.at[j - 1], tis_recv.at[j - 1], at_tis(j)
        )

    def from_tis(j):
        came = lax.rem(tis + (n_tis - j), n_tis)
        return remote(
            by_tis.at[tis], by_tis.at[came], tis_send.at[j - 1], tis_recv.at[j - 1], at_tis(j)
        )

    barrier = pltpu.get_barrier_semaphore()
    near = set(k % n_ctx for k in range(-SPAN, SPAN + 1)) | set(range(0, n_ctx, 2))
    peers = [at_ctx(k) for k in sorted(near) if k]
    peers += [at_tis(j) for j in range(1, n_tis)] + [at_rep(j) for j in range(1, n_rep)]
    for peer in peers:
        pl.semaphore_signal(barrier, inc=1, device_id=peer, device_id_type=MESH)
    pl.semaphore_wait(barrier, len(peers))

    for k in range(1, REACH):
        halo(k).start()

    window[0] = acc_ref[0]
    mpad[...] = jnp.zeros_like(mpad)
    mpad[:, 0:SLOTS] = mask_ref[0].astype(F32)
    row = lax.broadcasted_iota(jnp.int32, (WIDTH, WIDTH), 0)
    col = lax.broadcasted_iota(jnp.int32, (WIDTH, WIDTH), 1)
    per_core = WIDTH // 2
    per_rep = per_core // n_rep
    deep = per_rep // n_z
    want = (
        (((row // deep) % n_z) * 2 + row // per_core) * (WIDTH // n_ctx)
        + ((row // per_rep) % n_rep) * deep
        + row % deep
    )
    perm[...] = jnp.where(col == want, 2.0, 0.0).astype(BF16)
    for t in range(tissues):
        line = wo_ref[t : t + 1, :].astype(F32)
        out_cols[t] = jnp.broadcast_to(line, (LANES, HIDDEN)).astype(BF16)
        out_rows[t] = jnp.broadcast_to(0.5 * line, (8, HIDDEN))
        goals[t] = jnp.broadcast_to(goal_ref[0, :, t : t + 1], (BLK, LANES))
    losses[...] = jnp.zeros_like(losses)
    eye = lax.broadcasted_iota(jnp.int32, (BLK, BLK), 0) == lax.broadcasted_iota(
        jnp.int32, (BLK, BLK), 1
    )
    dcol = jnp.sum(
        jnp.where(eye, jnp.broadcast_to(dpos_ref[...].astype(F32), (BLK, BLK)), 0.0),
        axis=1,
        keepdims=True,
    )
    dcol = jnp.broadcast_to(dcol, (BLK, LANES)).astype(jnp.int32)
    lane = lax.broadcasted_iota(jnp.int32, (BLK, BLK, LANES), 2)
    slot_in = lax.broadcasted_iota(jnp.int32, (BLK, BLK, LANES), 0)
    ones = jnp.ones((LANES, LANES), BF16)
    donors = don_ref[0].astype(F32)

    def before(k):
        base = (ctx + k) * BLK
        dist = jnp.stack(
            [
                k * BLOCK_BP + apos_ref[0, lax.rem(base + a, n_ctx * BLK)] - dcol
                for a in range(BLK)
            ]
        )
        bins = jnp.clip(lax.shift_right_arithmetic(dist - 1, 11), 0, BINS - 1)
        lookup = jnp.where(bins == lane, 1.0, 0.0).astype(BF16).reshape(ROWS, BINS)
        table = jnp.dot(lookup, table_ref[...], preferred_element_type=F32)
        picked = jnp.where(lane == slot_in + k * BLK, mpad[...][None], 0.0)
        allowed = jnp.dot(
            picked.astype(BF16).reshape(ROWS, LANES), ones, preferred_element_type=F32
        ).reshape(BLK, BLK, LANES)
        exists = ctx + k < n_ctx
        ok = (allowed > 0.5) & (dist > 0) & (dist <= SPAN * BLOCK_BP)
        ok = jnp.where(ok, 1.0, 0.0)
        valid[pl.ds(k * BLK, BLK)] = jnp.where(exists, ok, 0.0)
        feats = jnp.where(exists, window[k].astype(F32), 0.0)
        pre = table.reshape(BLK, BLK, WIDTH) + donors[None] + feats[:, None, :]
        h = 0.5 * pre.reshape(ROWS, WIDTH)
        u = jnp.tanh(h)
        p = h * u
        pair = 0.5 * (h + p).astype(BF16).astype(F32)
        half = pair.astype(BF16)
        half_pair[pl.ds(pl.multiple_of(k * ROWS, ROWS), ROWS)] = half
        slope_pre[k] = 0.5 * ((1.0 + u) * ((1.0 + h) - p))
        flipped = lax.dot_general(
            perm[...], half, (((1,), (1,)), ((), ())), preferred_element_type=F32
        ).astype(BF16)
        pair_t[k] = flipped.reshape(2, per_core, ROWS)

    before(0)
    for k in range(1, REACH):
        halo(k).wait()

    def more(k, carry):
        before(k)
        return carry

    lax.fori_loop(1, REACH, more, 0)

    slot_all = lax.broadcasted_iota(jnp.int32, (SLOTS, BLK, LANES), 0)
    lane_row = lax.broadcasted_iota(jnp.int32, (BLK, LANES), 1)

    def send_rep(t):
        to_core(t).wait()
        total = part[t, core] + from_core[t]
        by_rep[t] = total.reshape(n_rep, per_rep, HIDDEN)
        for j in range(1, n_rep):
            to_rep(t, j).start()

    def send_z(t):
        for j in range(1, n_rep):
            to_rep(t, j).wait()
        total = by_rep[t, rep]
        for j in range(1, n_rep):
            total = total + from_rep[t, j - 1]
        for i in range(n_z):
            by_z[t, i] = total[i * deep : (i + 1) * deep]
        for j in range(1, n_z):
            to_z(t, j).start()

    def weight_grad(t, side):
        total = None
        for k in range(REACH):
            term = jnp.dot(
                pair_t[k, side],
                grad_hid[t, k * ROWS : (k + 1) * ROWS],
                preferred_element_type=F32,
            )
            total = term if total is None else total + term
        part[t, side] = total

    def tissue(t, carry):
        def forward(k, carry):
            rows = pl.ds(pl.multiple_of(k * ROWS, ROWS), ROWS)
            h = jnp.dot(half_pair[rows], w_ref[t], preferred_element_type=F32)
            u = jnp.tanh(h)
            p = h * u
            slope[rows] = (1.0 + u) * ((1.0 + h) - p)
            logit[pl.ds(k * BLK, BLK)] = lax.dot_general(
                (h + p).astype(BF16),
                out_cols[t],
                (((1,), (1,)), ((), ())),
                preferred_element_type=F32,
            ).reshape(BLK, BLK, LANES)
            return carry

        lax.fori_loop(0, REACH, forward, 0)

        @pl.when(t >= 1)
        def _():
            send_rep(t - 1)

        raw = logit[...]
        ok = valid[...] > 0.5
        top = jnp.maximum(jnp.max(jnp.where(ok, raw, -jnp.inf), axis=0), 0.0)
        expo = jnp.where(ok, jnp.exp(raw - top[None]), 0.0)
        total = jnp.sum(expo, axis=0) + jnp.exp(-top)
        hit = goals[t][None] == slot_all
        grad_logit[...] = expo * (1.0 / total)[None] - jnp.where(hit, 1.0, 0.0)
        seen = jnp.sum(jnp.where(hit, raw, 0.0), axis=0)
        losses[...] = jnp.where(lane_row == t, top + jnp.log(total) - seen, losses[...])

        def backward(k, carry):
            rows = pl.ds(pl.multiple_of(k * ROWS, ROWS), ROWS)
            gl = grad_logit[pl.ds(k * BLK, BLK)].reshape(ROWS, LANES)
            wide = jnp.concatenate([gl] * (HIDDEN // LANES), axis=1)
            grad_hid[t, rows] = ((wide * out_rows[t, 0:1]) * slope[rows]).astype(BF16)
            return carry

        lax.fori_loop(0, REACH, backward, 0)

        @pl.when(t >= 1)
        def _():
            send_z(t - 1)

        weight_grad(t, 1 - core)
        to_core(t).start()
        weight_grad(t, core)
        return carry

    lax.fori_loop(0, tissues, tissue, 0)
    last = tissues - 1
    send_rep(last)
    loss_ref[0] = losses[:, 0:tissues]

    def after(step, carry):
        k = SPAN - step
        rows = pl.ds(pl.multiple_of(k * ROWS, ROWS), ROWS)
        total = None
        for t in range(tissues):
            term = lax.dot_general(
                grad_hid[t, rows],
                w_ref[t],
                (((1,), (1,)), ((), ())),
                preferred_element_type=F32,
            )
            total = term if total is None else total + term
        grad_pre = (total * slope_pre[k]).reshape(BLK, BLK, WIDTH)
        contrib[k] = jnp.sum(grad_pre, axis=1)
        return carry

    lax.fori_loop(0, REACH, after, 0)
    for k in range(1, REACH):
        to_ctx(k).start()
    send_z(last)
    total = contrib[0]
    for k in range(1, REACH):
        to_ctx(k).wait()
        total = total + from_ctx[k - 1]
    by_tis[tis] = total
    for j in range(1, n_tis):
        to_tis(j).start()

    def finish(t, carry):
        total = by_z[t, z]
        for j in range(1, n_z):
            to_z(t, j).wait()
            total = total + from_z[t, j - 1]
        gw_ref[t] = total
        return carry

    lax.fori_loop(0, tissues, finish, 0)
    for j in range(1, n_tis):
        to_tis(j).wait_send()
        from_tis(j).wait_recv()
    total = by_tis[0]
    for j in range(1, n_tis):
        total = total + by_tis[j]
    gacc_ref[0] = total


def solution(mesh):
    n_ctx, n_tis, n_rep = (mesh.shape[name] for name in ("ctx", "tis", "rep"))
    n_z = n_ctx // 2

    def on_device(don, acc, dpos, apos, mask, goal, table, w, wo):
        tissues = w.shape[0]
        per_core = WIDTH // 2
        per_rep = per_core // n_rep
        deep = per_rep // n_z
        vmem = pl.BlockSpec(memory_space=pltpu.VMEM)
        smem = pl.BlockSpec(memory_space=pltpu.SMEM)
        pairs = SLOTS * BLK
        scratch = [
            pltpu.VMEM((REACH, BLK, WIDTH), BF16),
            pltpu.VMEM((BLK, LANES), F32),
            pltpu.VMEM((WIDTH, WIDTH), BF16),
            pltpu.VMEM((pairs, WIDTH), BF16),
            pltpu.VMEM((REACH, 2, per_core, ROWS), BF16),
            pltpu.VMEM((REACH, ROWS, WIDTH), F32),
            pltpu.VMEM((SLOTS, BLK, LANES), F32),
            pltpu.VMEM((pairs, HIDDEN), F32),
            pltpu.VMEM((SLOTS, BLK, LANES), F32),
            pltpu.VMEM((SLOTS, BLK, LANES), F32),
            pltpu.VMEM((tissues, pairs, HIDDEN), BF16),
            pltpu.VMEM((tissues, LANES, HIDDEN), BF16),
            pltpu.VMEM((tissues, 8, HIDDEN), F32),
            pltpu.VMEM((tissues, BLK, LANES), jnp.int32),
            pltpu.VMEM((BLK, LANES), F32),
            pltpu.VMEM((tissues, 2, per_core, HIDDEN), F32),
            pltpu.VMEM((tissues, per_core, HIDDEN), F32),
            pltpu.VMEM((tissues, n_rep, per_rep, HIDDEN), F32),
            pltpu.VMEM((tissues, n_rep - 1, per_rep, HIDDEN), F32),
            pltpu.VMEM((tissues, n_z, deep, HIDDEN), F32),
            pltpu.VMEM((tissues, n_z - 1, deep, HIDDEN), F32),
            pltpu.VMEM((REACH, BLK, WIDTH), F32),
            pltpu.VMEM((SPAN, BLK, WIDTH), F32),
            pltpu.VMEM((n_tis, BLK, WIDTH), F32),
            pltpu.SemaphoreType.DMA((SPAN,)),
            pltpu.SemaphoreType.DMA((SPAN,)),
            pltpu.SemaphoreType.DMA((tissues,)),
            pltpu.SemaphoreType.DMA((tissues,)),
            pltpu.SemaphoreType.DMA((tissues, n_rep - 1)),
            pltpu.SemaphoreType.DMA((tissues, n_rep - 1)),
            pltpu.SemaphoreType.DMA((tissues, n_z - 1)),
            pltpu.SemaphoreType.DMA((tissues, n_z - 1)),
            pltpu.SemaphoreType.DMA((SPAN,)),
            pltpu.SemaphoreType.DMA((SPAN,)),
            pltpu.SemaphoreType.DMA((n_tis - 1,)),
            pltpu.SemaphoreType.DMA((n_tis - 1,)),
        ]
        return pl.pallas_call(
            functools.partial(kernel, (n_ctx, n_tis, n_rep, tissues)),
            out_shape=(
                jax.ShapeDtypeStruct((1, BLK, tissues), F32),
                jax.ShapeDtypeStruct((tissues, deep, HIDDEN), F32),
                jax.ShapeDtypeStruct((1, BLK, WIDTH), F32),
            ),
            in_specs=[vmem, vmem, vmem, smem, vmem, vmem, vmem, vmem, vmem],
            out_specs=(vmem, vmem, vmem),
            scratch_shapes=scratch,
            compiler_params=pltpu.CompilerParams(
                collective_id=0, has_side_effects=True, vmem_limit_bytes=44 << 20
            ),
        )(don, acc, dpos, apos, mask, goal, table, w, wo)

    placed = (
        P("rep", "ctx", None),
        P("rep", "ctx", None),
        P("rep", "ctx"),
        P("rep", None),
        P("rep", "ctx", None),
        P("rep", "ctx", "tis"),
        P(),
        P("tis", None, None),
        P("tis", None),
    )
    return jax.shard_map(
        on_device,
        mesh=mesh,
        in_specs=placed,
        out_specs=(P("rep", "ctx", "tis"), P("tis", ("ctx", "rep"), None), P("rep", "ctx", None)),
        check_vma=False,
    )
```

time: 282 us -> 70.3 us (0.25)
  waiting for transfers between devices: 172 us -> 0 us
  Pallas kernels: 0 us -> 62.4 us
  starting transfers between devices: 25.8 us -> 0 us
  blocking collectives: 22.4 us -> 0 us
  matrix products: 20.5 us -> 0 us
  other arithmetic: 15.4 us -> 0 us
  between operations: 15.1 us -> 0.68 us
    unnamed x2 -> x0, waiting for transfers between devices: 161 us -> none
    pallas_call x0 -> x1, Pallas kernels: none -> 62.4 us  [on_device(): pl.pallas_call(functools.partial(kernel, (n_ctx, n_tis, n_rep, tissues)),...]
    ppermute x8 -> x0, starting transfers between devices: 25.8 us -> none  [passed_along(): lax.ppermute(value, axis, [(source, source + steps) for source in range(f...]
    psum x1 -> x0, blocking collectives: 22.4 us -> none  [on_device(): grad_acceptor = lax.psum(carried, 'tis')]
    dot_general x17 -> x0, matrix products: 20.5 us -> none  [the longest x4 7.74 us: on_device(): hid = jnp.dot(flat, w_in, preferred_element_type=jnp.float32)]
    ppermute x8 -> x0, waiting for transfers between devices: 10.5 us -> none  [passed_along(): lax.ppermute(value, axis, [(source, source + steps) for source in range(f...]
    convert_element_type x5 -> x0, other arithmetic: 9.16 us -> none  [the longest x4 9.15 us: on_device(): grad_hid = (grad_act * silu_grad(hid)).astype(jnp.bfloat16)]
    unnamed x29 -> x19, local copies, waits for them, and re-layouts: 3.83 us -> 6.15 us
  transfers between devices with their start and end apart: 9 -> 0, of which waited for: 6 -> 0; matrix products, arithmetic and copies ran while one was open for 4% -> 0% of each run, Pallas kernels for 0% -> 0%
where the time goes in v1:
time: 70.3 us; the launch traced here: 69.9 us
  Pallas kernels  62.4 us (89%)
  local copies, waits for them, and re-layouts  6.8 us (10%)
    pallas_call x1, Pallas kernels, on_device(): pl.pallas_call(functools.partial(kernel, (n_ctx, n_tis, n_rep, tissues)),...  62.4 us
    unnamed x19, local copies, waits for them, and re-layouts  6.15 us

profile of v1, /device:TPU:1, one launch (start us, length us, event | category | flops | bytes accessed | tf_op | source)
XLA Modules:
  0.0 69.9 jit_solution(1765676202689344728)
XLA Ops:
  0.6 0.0 copy-start.6
  0.6 0.0 copy-start.7
  0.7 0.0 copy-start.2
  0.7 0.8 %copy.12.goal_ref = s32[1,16,4]{2,1,0:T(8,128)S(1)} copy(s32[1,16,4]{1,2,0:T(4,128)} %param.14) | data formatting | bytes 512 | tf_op args[5]
  1.4 0.0 copy-done.6
  1.4 0.0 copy-done.7
  1.4 0.0 copy-done.2
  1.4 0.0 copy-start
  1.5 1.2 %copy-done = bf16[4,256,512]{2,1,0:T(8,128)(2,1)S(1)} copy-done((bf16[4,256,512]{2,1,0:T(8,128)(2,1)S(1)}, bf16[4,256,512]{2,1,0:T(8,128)(2,1)}, u32[]{:S(2)}) %copy-start) | copy-done | bytes 1048600
  2.7 0.0 copy-start.1
  2.7 0.8 %copy-done.1 = bf16[128,256]{1,0:T(8,128)(2,1)S(1)} copy-done((bf16[128,256]{1,0:T(8,128)(2,1)S(1)}, bf16[128,256]{1,0:T(8,128)(2,1)}, u32[]{:S(2)}) %copy-start.1) | copy-done | bytes 65560
  3.5 0.0 copy-start.3
  3.5 0.7 copy-done.3
  4.2 0.0 copy-start.4
  4.2 0.7 copy-done.4
  4.9 0.0 copy-start.5
  4.9 0.7 copy-done.5
  5.6 62.4 %shard_map.112 = (f32[1,16,4]{2,1,0:T(8,128)S(1)}, f32[4,4,512]{2,1,0:T(4,128)S(1)}, f32[1,16,256]{2,1,0:T(8,128)S(1)}) custom-call(bf16[1,16,256]{2,1,0:T(8,128)(2,1)S(1)} %copy-done.2, bf16[1,16,256]{2,1,0:T(8,128)(2,1)S(1)} %copy-done.3, s32[1,16]{1,0:T(1,128)S(1)} %copy-done.7, s32[1,256]{1,0:T(1,128)S(1)} %copy-done.6, s32[1,16,80]{2,1,0:T(8,128)S(1)} %copy-done.4, ...), custom_call_target="tpu_custom_call" | custom-call | tf_op jit(solution)/shard_map/pallas_call | solution.py:420
  68.0 0.7 copy.13
  68.7 0.6 copy.16
  69.3 0.6 copy.17
Async XLA Ops:
  0.6 0.8 %copy-start.6 = (s32[1,256]{1,0:T(1,128)S(1)}, s32[1,256]{1,0:T(1,128)}, u32[]{:S(2)}) copy-start(s32[1,256]{1,0:T(1,128)} %apos_ref.1) | copy-start | bytes 3076
  0.6 0.8 %copy-start.7 = (s32[1,16]{1,0:T(1,128)S(1)}, s32[1,16]{1,0:T(1,128)}, u32[]{:S(2)}) copy-start(s32[1,16]{1,0:T(1,128)} %dpos_ref.1) | copy-start | bytes 196
  0.7 0.8 %copy-start.2 = (bf16[1,16,256]{2,1,0:T(8,128)(2,1)S(1)}, bf16[1,16,256]{2,1,0:T(8,128)(2,1)}, u32[]{:S(2)}) copy-start(bf16[1,16,256]{2,1,0:T(8,128)(2,1)} %don_ref.1) | copy-start | bytes 24580
  1.4 1.2 %copy-start = (bf16[4,256,512]{2,1,0:T(8,128)(2,1)S(1)}, bf16[4,256,512]{2,1,0:T(8,128)(2,1)}, u32[]{:S(2)}) copy-start(bf16[4,256,512]{2,1,0:T(8,128)(2,1)} %w_ref.1) | copy-start | bytes 3145732
  2.7 0.8 %copy-start.1 = (bf16[128,256]{1,0:T(8,128)(2,1)S(1)}, bf16[128,256]{1,0:T(8,128)(2,1)}, u32[]{:S(2)}) copy-start(bf16[128,256]{1,0:T(8,128)(2,1)} %table_ref.1) | copy-start | bytes 196612
  3.5 0.7 copy-start.3
  4.2 0.7 copy-start.4
  4.9 0.7 copy-start.5

commit v2 on v1

--- a/solution.py
+++ b/solution.py
@@ -21,12 +21,24 @@
 WIDTH = 256
 HIDDEN = 512
 LANES = 128
+CHUNK = 640
 
 
 def kernel(
     sizes,
+    don_in,
+    acc_in,
+    dpos_in,
+    apos_in,
+    mask_in,
+    goal_in,
+    table_in,
+    w_in,
+    wo_in,
+    loss_ref,
+    gw_ref,
+    gacc_ref,
     don_ref,
-    acc_ref,
     dpos_ref,
     apos_ref,
     mask_ref,
@@ -34,9 +46,6 @@
     table_ref,
     w_ref,
     wo_ref,
-    loss_ref,
-    gw_ref,
-    gacc_ref,
     window,
     mpad,
     perm,
@@ -55,18 +64,22 @@
     part,
     from_core,
     by_rep,
-    from_rep,
+    from_first,
+    from_second,
     by_z,
     from_z,
     contrib,
     from_ctx,
     by_tis,
+    local,
     halo_send,
     halo_recv,
     core_send,
     core_recv,
-    rep_send,
-    rep_recv,
+    first_send,
+    first_recv,
+    second_send,
+    second_recv,
     z_send,
     z_recv,
     ctx_send,
@@ -105,7 +118,7 @@
 
     def halo(k):
         return remote(
-            acc_ref.at[0], window.at[k], halo_send.at[k - 1], halo_recv.at[k - 1], at_ctx(-k)
+            acc_in.at[0], window.at[k], halo_send.at[k - 1], halo_recv.at[k - 1], at_ctx(-k)
         )
 
     def to_core(t):
@@ -113,13 +126,25 @@
             part.at[t, 1 - core], from_core.at[t], core_send.at[t], core_recv.at[t], other_core
         )
 
-    def to_rep(t, j):
-        return remote(
-            by_rep.at[t, lax.rem(rep + j, n_rep)],
-            from_rep.at[t, j - 1],
-            rep_send.at[t, j - 1],
-            rep_recv.at[t, j - 1],
-            at_rep(j),
+    flip = (rep + 1 - 2 * lax.rem(rep, 2), n_rep - 1 - rep)
+    far = lax.rem(rep + 2, n_rep)
+
+    def to_first(t, half):
+        return remote(
+            by_rep.at[t, half, pl.ds(2, 2)],
+            from_first.at[t, half],
+            first_send.at[t, half],
+            first_recv.at[t, half],
+            {"rep": flip[half]},
+        )
+
+    def to_second(t, half):
+        return remote(
+            by_rep.at[t, half, 1],
+            from_second.at[t, half],
+            second_send.at[t, half],
+            second_recv.at[t, half],
+            {"rep": flip[1 - half]},
         )
 
     def to_z(t, j):
@@ -146,6 +171,25 @@
         return remote(
             by_tis.at[tis], by_tis.at[came], tis_send.at[j - 1], tis_recv.at[j - 1], at_tis(j)
         )
+
+    staged = [
+        pltpu.make_async_copy(src, dst, local.at[i])
+        for i, (src, dst) in enumerate(
+            [
+                (apos_in, apos_ref),
+                (dpos_in, dpos_ref),
+                (don_in, don_ref),
+                (acc_in.at[0], window.at[0]),
+                (mask_in, mask_ref),
+                (table_in, table_ref),
+                (wo_in, wo_ref),
+                (goal_in, goal_ref),
+                (w_in, w_ref),
+            ]
+        )
+    ]
+    for copy in staged:
+        copy.start()
 
     barrier = pltpu.get_barrier_semaphore()
     near = set(k % n_ctx for k in range(-SPAN, SPAN + 1)) | set(range(0, n_ctx, 2))
@@ -158,7 +202,8 @@
     for k in range(1, REACH):
         halo(k).start()
 
-    window[0] = acc_ref[0]
+    for copy in staged[:-1]:
+        copy.wait()
     mpad[...] = jnp.zeros_like(mpad)
     mpad[:, 0:SLOTS] = mask_ref[0].astype(F32)
     row = lax.broadcasted_iota(jnp.int32, (WIDTH, WIDTH), 0)
@@ -176,17 +221,18 @@
         line = wo_ref[t : t + 1, :].astype(F32)
         out_cols[t] = jnp.broadcast_to(line, (LANES, HIDDEN)).astype(BF16)
         out_rows[t] = jnp.broadcast_to(0.5 * line, (8, HIDDEN))
-        goals[t] = jnp.broadcast_to(goal_ref[0, :, t : t + 1], (BLK, LANES))
-    losses[...] = jnp.zeros_like(losses)
     eye = lax.broadcasted_iota(jnp.int32, (BLK, BLK), 0) == lax.broadcasted_iota(
         jnp.int32, (BLK, BLK), 1
     )
-    dcol = jnp.sum(
-        jnp.where(eye, jnp.broadcast_to(dpos_ref[...].astype(F32), (BLK, BLK)), 0.0),
-        axis=1,
-        keepdims=True,
-    )
-    dcol = jnp.broadcast_to(dcol, (BLK, LANES)).astype(jnp.int32)
+
+    def column(line):
+        spread = jnp.where(eye, jnp.broadcast_to(line.astype(F32), (BLK, BLK)), 0.0)
+        total = jnp.sum(spread, axis=1, keepdims=True)
+        return jnp.broadcast_to(total, (BLK, LANES)).astype(jnp.int32)
+
+    dcol = column(dpos_ref[...])
+    for t in range(tissues):
+        goals[t] = column(goal_ref[0, t : t + 1, :])
     lane = lax.broadcasted_iota(jnp.int32, (BLK, BLK, LANES), 2)
     slot_in = lax.broadcasted_iota(jnp.int32, (BLK, BLK, LANES), 0)
     ones = jnp.ones((LANES, LANES), BF16)
@@ -219,11 +265,11 @@
         pair = 0.5 * (h + p).astype(BF16).astype(F32)
         half = pair.astype(BF16)
         half_pair[pl.ds(pl.multiple_of(k * ROWS, ROWS), ROWS)] = half
-        slope_pre[k] = 0.5 * ((1.0 + u) * ((1.0 + h) - p))
+        slope_pre[pl.ds(pl.multiple_of(k * ROWS, ROWS), ROWS)] = 0.5 * ((1.0 + u) * ((1.0 + h) - p))
         flipped = lax.dot_general(
             perm[...], half, (((1,), (1,)), ((), ())), preferred_element_type=F32
         ).astype(BF16)
-        pair_t[k] = flipped.reshape(2, per_core, ROWS)
+        pair_t[:, pl.ds(pl.multiple_of(k * ROWS, ROWS), ROWS)] = flipped
 
     before(0)
     for k in range(1, REACH):
@@ -238,55 +284,61 @@
     slot_all = lax.broadcasted_iota(jnp.int32, (SLOTS, BLK, LANES), 0)
     lane_row = lax.broadcasted_iota(jnp.int32, (BLK, LANES), 1)
 
-    def send_rep(t):
+    def send_first(t):
         to_core(t).wait()
-        total = part[t, core] + from_core[t]
-        by_rep[t] = total.reshape(n_rep, per_rep, HIDDEN)
-        for j in range(1, n_rep):
-            to_rep(t, j).start()
+        for half in range(2):
+            for i, q in enumerate((rep, flip[1 - half], flip[half], far)):
+                rows = pl.ds(pl.multiple_of(q * per_rep, per_rep), per_rep)
+                by_rep[t, half, i] = part[t, core, half, rows] + from_core[t, half, rows]
+            to_first(t, half).start()
+
+    def send_second(t):
+        for half in range(2):
+            to_first(t, half).wait()
+            by_rep[t, half, 1] = by_rep[t, half, 1] + from_first[t, half, 1]
+            to_second(t, half).start()
 
     def send_z(t):
-        for j in range(1, n_rep):
-            to_rep(t, j).wait()
-        total = by_rep[t, rep]
-        for j in range(1, n_rep):
-            total = total + from_rep[t, j - 1]
-        for i in range(n_z):
-            by_z[t, i] = total[i * deep : (i + 1) * deep]
+        for half in range(2):
+            to_second(t, half).wait()
+            total = by_rep[t, half, 0] + from_first[t, half, 0] + from_second[t, half]
+            for i in range(n_z):
+                by_z[t, i, :, half * WIDTH : (half + 1) * WIDTH] = total[i * deep : (i + 1) * deep]
         for j in range(1, n_z):
             to_z(t, j).start()
 
-    def weight_grad(t, side):
-        total = None
-        for k in range(REACH):
-            term = jnp.dot(
-                pair_t[k, side],
-                grad_hid[t, k * ROWS : (k + 1) * ROWS],
-                preferred_element_type=F32,
-            )
-            total = term if total is None else total + term
-        part[t, side] = total
+    def weight_grad(t):
+        total = jnp.dot(pair_t[...], grad_hid[t], preferred_element_type=F32)
+        total = total.reshape(2, per_core, HIDDEN)
+        part[t, :, 0] = total[:, :, :WIDTH]
+        part[t, :, 1] = total[:, :, WIDTH:]
+
+    staged[-1].wait()
 
     def tissue(t, carry):
         def forward(k, carry):
-            rows = pl.ds(pl.multiple_of(k * ROWS, ROWS), ROWS)
+            rows = pl.ds(pl.multiple_of(k * CHUNK, CHUNK), CHUNK)
             h = jnp.dot(half_pair[rows], w_ref[t], preferred_element_type=F32)
             u = jnp.tanh(h)
             p = h * u
             slope[rows] = (1.0 + u) * ((1.0 + h) - p)
-            logit[pl.ds(k * BLK, BLK)] = lax.dot_general(
+            logit[pl.ds(k * (CHUNK // BLK), CHUNK // BLK)] = lax.dot_general(
                 (h + p).astype(BF16),
                 out_cols[t],
                 (((1,), (1,)), ((), ())),
                 preferred_element_type=F32,
-            ).reshape(BLK, BLK, LANES)
+            ).reshape(CHUNK // BLK, BLK, LANES)
             return carry
 
-        lax.fori_loop(0, REACH, forward, 0)
+        lax.fori_loop(0, SLOTS * BLK // CHUNK, forward, 0)
 
         @pl.when(t >= 1)
         def _():
-            send_rep(t - 1)
+            send_first(t - 1)
+
+        @pl.when(t >= 2)
+        def _():
+            send_second(t - 2)
 
         raw = logit[...]
         ok = valid[...] > 0.5
@@ -296,7 +348,7 @@
         hit = goals[t][None] == slot_all
         grad_logit[...] = expo * (1.0 / total)[None] - jnp.where(hit, 1.0, 0.0)
         seen = jnp.sum(jnp.where(hit, raw, 0.0), axis=0)
-        losses[...] = jnp.where(lane_row == t, top + jnp.log(total) - seen, losses[...])
+        losses[t] = top + jnp.log(total) - seen
 
         def backward(k, carry):
             rows = pl.ds(pl.multiple_of(k * ROWS, ROWS), ROWS)
@@ -307,23 +359,21 @@
 
         lax.fori_loop(0, REACH, backward, 0)
 
-        @pl.when(t >= 1)
+        weight_grad(t)
+        to_core(t).start()
+
+        @pl.when(t >= 2)
         def _():
-            send_z(t - 1)
-
-        weight_grad(t, 1 - core)
-        to_core(t).start()
-        weight_grad(t, core)
+            send_z(t - 2)
+
         return carry
 
     lax.fori_loop(0, tissues, tissue, 0)
     last = tissues - 1
-    send_rep(last)
-    loss_ref[0] = losses[:, 0:tissues]
-
-    def after(step, carry):
-        k = SPAN - step
-        rows = pl.ds(pl.multiple_of(k * ROWS, ROWS), ROWS)
+    send_second(last - 1)
+
+    def after(low, high):
+        rows = slice(low * ROWS, high * ROWS)
         total = None
         for t in range(tissues):
             term = lax.dot_general(
@@ -333,13 +383,16 @@
                 preferred_element_type=F32,
             )
             total = term if total is None else total + term
-        grad_pre = (total * slope_pre[k]).reshape(BLK, BLK, WIDTH)
-        contrib[k] = jnp.sum(grad_pre, axis=1)
-        return carry
-
-    lax.fori_loop(0, REACH, after, 0)
-    for k in range(1, REACH):
-        to_ctx(k).start()
+        grad_pre = (total * slope_pre[rows]).reshape((high - low) * BLK, BLK, WIDTH)
+        contrib[low:high] = jnp.sum(grad_pre, axis=1).reshape(high - low, BLK, WIDTH)
+        for k in range(max(low, 1), high):
+            to_ctx(k).start()
+
+    send_first(last)
+    after(3, REACH)
+    send_z(last - 1)
+    send_second(last)
+    after(0, 3)
     send_z(last)
     total = contrib[0]
     for k in range(1, REACH):
@@ -348,6 +401,10 @@
     by_tis[tis] = total
     for j in range(1, n_tis):
         to_tis(j).start()
+    wide_eye = lax.broadcasted_iota(jnp.int32, (BLK, LANES), 0) == lane_row
+    for t in range(tissues):
+        line = jnp.sum(jnp.where(wide_eye, losses[t], 0.0), axis=0, keepdims=True)
+        loss_ref[0, t : t + 1, :] = line[:, 0:BLK]
 
     def finish(t, carry):
         total = by_z[t, z]
@@ -377,15 +434,23 @@
         per_rep = per_core // n_rep
         deep = per_rep // n_z
         vmem = pl.BlockSpec(memory_space=pltpu.VMEM)
-        smem = pl.BlockSpec(memory_space=pltpu.SMEM)
+        hbm = pl.BlockSpec(memory_space=pltpu.HBM)
         pairs = SLOTS * BLK
         scratch = [
+            pltpu.VMEM((1, BLK, WIDTH), BF16),
+            pltpu.VMEM((1, BLK), jnp.int32),
+            pltpu.SMEM((1, n_ctx * BLK), jnp.int32),
+            pltpu.VMEM((1, BLK, SLOTS), jnp.int32),
+            pltpu.VMEM((1, tissues, BLK), jnp.int32),
+            pltpu.VMEM((BINS, WIDTH), BF16),
+            pltpu.VMEM((tissues, WIDTH, HIDDEN), BF16),
+            pltpu.VMEM((tissues, HIDDEN), BF16),
             pltpu.VMEM((REACH, BLK, WIDTH), BF16),
             pltpu.VMEM((BLK, LANES), F32),
             pltpu.VMEM((WIDTH, WIDTH), BF16),
             pltpu.VMEM((pairs, WIDTH), BF16),
-            pltpu.VMEM((REACH, 2, per_core, ROWS), BF16),
-            pltpu.VMEM((REACH, ROWS, WIDTH), F32),
+            pltpu.VMEM((WIDTH, pairs), BF16),
+            pltpu.VMEM((pairs, WIDTH), F32),
             pltpu.VMEM((SLOTS, BLK, LANES), F32),
             pltpu.VMEM((pairs, HIDDEN), F32),
             pltpu.VMEM((SLOTS, BLK, LANES), F32),
@@ -394,22 +459,26 @@
             pltpu.VMEM((tissues, LANES, HIDDEN), BF16),
             pltpu.VMEM((tissues, 8, HIDDEN), F32),
             pltpu.VMEM((tissues, BLK, LANES), jnp.int32),
-            pltpu.VMEM((BLK, LANES), F32),
-            pltpu.VMEM((tissues, 2, per_core, HIDDEN), F32),
-            pltpu.VMEM((tissues, per_core, HIDDEN), F32),
-            pltpu.VMEM((tissues, n_rep, per_rep, HIDDEN), F32),
-            pltpu.VMEM((tissues, n_rep - 1, per_rep, HIDDEN), F32),
+            pltpu.VMEM((tissues, BLK, LANES), F32),
+            pltpu.VMEM((tissues, 2, 2, per_core, WIDTH), F32),
+            pltpu.VMEM((tissues, 2, per_core, WIDTH), F32),
+            pltpu.VMEM((tissues, 2, n_rep, per_rep, WIDTH), F32),
+            pltpu.VMEM((tissues, 2, 2, per_rep, WIDTH), F32),
+            pltpu.VMEM((tissues, 2, per_rep, WIDTH), F32),
             pltpu.VMEM((tissues, n_z, deep, HIDDEN), F32),
             pltpu.VMEM((tissues, n_z - 1, deep, HIDDEN), F32),
             pltpu.VMEM((REACH, BLK, WIDTH), F32),
             pltpu.VMEM((SPAN, BLK, WIDTH), F32),
             pltpu.VMEM((n_tis, BLK, WIDTH), F32),
+            pltpu.SemaphoreType.DMA((9,)),
             pltpu.SemaphoreType.DMA((SPAN,)),
             pltpu.SemaphoreType.DMA((SPAN,)),
             pltpu.SemaphoreType.DMA((tissues,)),
             pltpu.SemaphoreType.DMA((tissues,)),
-            pltpu.SemaphoreType.DMA((tissues, n_rep - 1)),
-            pltpu.SemaphoreType.DMA((tissues, n_rep - 1)),
+            pltpu.SemaphoreType.DMA((tissues, 2)),
+            pltpu.SemaphoreType.DMA((tissues, 2)),
+            pltpu.SemaphoreType.DMA((tissues, 2)),
+            pltpu.SemaphoreType.DMA((tissues, 2)),
             pltpu.SemaphoreType.DMA((tissues, n_z - 1)),
             pltpu.SemaphoreType.DMA((tissues, n_z - 1)),
             pltpu.SemaphoreType.DMA((SPAN,)),
@@ -417,20 +486,21 @@
             pltpu.SemaphoreType.DMA((n_tis - 1,)),
             pltpu.SemaphoreType.DMA((n_tis - 1,)),
         ]
-        return pl.pallas_call(
+        loss, grad_hidden, grad_acceptor = pl.pallas_call(
             functools.partial(kernel, (n_ctx, n_tis, n_rep, tissues)),
             out_shape=(
-                jax.ShapeDtypeStruct((1, BLK, tissues), F32),
+                jax.ShapeDtypeStruct((1, tissues, BLK), F32),
                 jax.ShapeDtypeStruct((tissues, deep, HIDDEN), F32),
                 jax.ShapeDtypeStruct((1, BLK, WIDTH), F32),
             ),
-            in_specs=[vmem, vmem, vmem, smem, vmem, vmem, vmem, vmem, vmem],
+            in_specs=[hbm] * 9,
             out_specs=(vmem, vmem, vmem),
             scratch_shapes=scratch,
             compiler_params=pltpu.CompilerParams(
-                collective_id=0, has_side_effects=True, vmem_limit_bytes=44 << 20
+                collective_id=0, has_side_effects=True, vmem_limit_bytes=60 << 20
             ),
-        )(don, acc, dpos, apos, mask, goal, table, w, wo)
+        )(don, acc, dpos, apos, mask, jnp.swapaxes(goal, 1, 2), table, w, wo)
+        return jnp.swapaxes(loss, 1, 2), grad_hidden, grad_acceptor
 
     placed = (
         P("rep", "ctx", None),

time: 70.3 us -> 56.2 us (0.80)
  Pallas kernels: 62.4 us -> 52 us
  local copies, waits for them, and re-layouts: 6.8 us -> 3.25 us
    pallas_call x1, Pallas kernels: 62.4 us -> 52 us  [on_device(): pl.pallas_call(functools.partial(kernel, (n_ctx, n_tis, n_rep, tissues)),...]
    unnamed x19 -> x7, local copies, waits for them, and re-layouts: 6.15 us -> 3.25 us
where the time goes in v2:
time: 56.2 us; the launch traced here: 55.9 us
  Pallas kernels  52 us (93%)
  local copies, waits for them, and re-layouts  3.25 us (6%)
  between operations  0.65 us (1%)
    pallas_call x1, Pallas kernels, on_device(): pl.pallas_call(functools.partial(kernel, (n_ctx, n_tis, n_rep, tissues)),...  52 us
    unnamed x7, local copies, waits for them, and re-layouts  3.25 us

profile of v2, /device:TPU:1, one launch (start us, length us, event | category | flops | bytes accessed | tf_op | source)
XLA Modules:
  0.0 55.9 jit_solution(3753723800609747929)
XLA Ops:
  0.6 52.0 %shard_map.112 = (f32[1,4,16]{2,1,0:T(4,128)}, f32[4,4,512]{2,1,0:T(4,128)}, f32[1,16,256]{2,1,0:T(8,128)}) custom-call(bf16[1,16,256]{2,1,0:T(8,128)(2,1)} %don_in.1, bf16[1,16,256]{2,1,0:T(8,128)(2,1)} %acc_in.1, s32[1,16]{1,0:T(1,128)} %dpos_in.1, s32[1,256]{1,0:T(1,128)} %apos_in.1, s32[1,16,80]{2,1,0:T(8,128)} %mask_in.1, s32[1,4,16]{2,1,0:T(4,128)} %bitcast.2, ...), custom_call_target="tpu_custom_call" | custom-call | tf_op jit(solution)/shard_map/pallas_call | solution.py:489
  52.7 0.0 copy-start.1
  52.7 0.7 %copy-done.1 = f32[1,4,16]{2,1,0:T(4,128)S(1)} copy-done((f32[1,4,16]{2,1,0:T(4,128)S(1)}, f32[1,4,16]{2,1,0:T(4,128)}, u32[]{:S(2)}) %copy-start.1) | copy-done | bytes 280
  53.3 0.6 %copy.15 = f32[1,16,4]{1,2,0:T(4,128)} copy(f32[1,16,4]{1,2,0:T(4,128)S(1)} %bitcast.3) | data formatting | bytes 512
  53.9 0.0 copy-start
  53.9 1.4 %copy.16 = f32[4,4,512]{2,1,0:T(4,128)} copy(f32[4,4,512]{2,1,0:T(4,128)} %get-tuple-element.13) | data formatting | bytes 65536
  55.3 0.0 copy-done
  55.3 0.6 %copy.17 = f32[1,16,256]{2,1,0:T(8,128)} copy(f32[1,16,256]{2,1,0:T(8,128)S(1)} %copy-done) | data formatting | bytes 32768
Async XLA Ops:
  52.7 0.7 %copy-start.1 = (f32[1,4,16]{2,1,0:T(4,128)S(1)}, f32[1,4,16]{2,1,0:T(4,128)}, u32[]{:S(2)}) copy-start(f32[1,4,16]{2,1,0:T(4,128)} %get-tuple-element.6) | copy-start | bytes 772
  53.9 1.4 %copy-start = (f32[1,16,256]{2,1,0:T(8,128)S(1)}, f32[1,16,256]{2,1,0:T(8,128)}, u32[]{:S(2)}) copy-start(f32[1,16,256]{2,1,0:T(8,128)} %get-tuple-element.14) | copy-start | bytes 49156

commit v3 on v2

--- a/solution.py
+++ b/solution.py
@@ -51,7 +51,7 @@
     perm,
     half_pair,
     pair_t,
-    slope_pre,
+    half_pre,
     valid,
     slope,
     logit,
@@ -197,11 +197,6 @@
     peers += [at_tis(j) for j in range(1, n_tis)] + [at_rep(j) for j in range(1, n_rep)]
     for peer in peers:
         pl.semaphore_signal(barrier, inc=1, device_id=peer, device_id_type=MESH)
-    pl.semaphore_wait(barrier, len(peers))
-
-    for k in range(1, REACH):
-        halo(k).start()
-
     for copy in staged[:-1]:
         copy.wait()
     mpad[...] = jnp.zeros_like(mpad)
@@ -233,6 +228,11 @@
     dcol = column(dpos_ref[...])
     for t in range(tissues):
         goals[t] = column(goal_ref[0, t : t + 1, :])
+    pl.semaphore_wait(barrier, len(peers))
+
+    for k in reversed(range(1, REACH)):
+        halo(k).start()
+
     lane = lax.broadcasted_iota(jnp.int32, (BLK, BLK, LANES), 2)
     slot_in = lax.broadcasted_iota(jnp.int32, (BLK, BLK, LANES), 0)
     ones = jnp.ones((LANES, LANES), BF16)
@@ -265,17 +265,16 @@
         pair = 0.5 * (h + p).astype(BF16).astype(F32)
         half = pair.astype(BF16)
         half_pair[pl.ds(pl.multiple_of(k * ROWS, ROWS), ROWS)] = half
-        slope_pre[pl.ds(pl.multiple_of(k * ROWS, ROWS), ROWS)] = 0.5 * ((1.0 + u) * ((1.0 + h) - p))
+        half_pre[pl.ds(pl.multiple_of(k * ROWS, ROWS), ROWS)] = h
         flipped = lax.dot_general(
             perm[...], half, (((1,), (1,)), ((), ())), preferred_element_type=F32
         ).astype(BF16)
         pair_t[:, pl.ds(pl.multiple_of(k * ROWS, ROWS), ROWS)] = flipped
 
     before(0)
-    for k in range(1, REACH):
+
+    def more(k, carry):
         halo(k).wait()
-
-    def more(k, carry):
         before(k)
         return carry
 
@@ -316,29 +315,25 @@
     staged[-1].wait()
 
     def tissue(t, carry):
-        def forward(k, carry):
-            rows = pl.ds(pl.multiple_of(k * CHUNK, CHUNK), CHUNK)
+        def forward(k):
+            rows = slice(k * CHUNK, (k + 1) * CHUNK)
             h = jnp.dot(half_pair[rows], w_ref[t], preferred_element_type=F32)
             u = jnp.tanh(h)
             p = h * u
             slope[rows] = (1.0 + u) * ((1.0 + h) - p)
-            logit[pl.ds(k * (CHUNK // BLK), CHUNK // BLK)] = lax.dot_general(
+            logit[k * (CHUNK // BLK) : (k + 1) * (CHUNK // BLK)] = lax.dot_general(
                 (h + p).astype(BF16),
                 out_cols[t],
                 (((1,), (1,)), ((), ())),
                 preferred_element_type=F32,
             ).reshape(CHUNK // BLK, BLK, LANES)
-            return carry
-
-        lax.fori_loop(0, SLOTS * BLK // CHUNK, forward, 0)
-
-        @pl.when(t >= 1)
+
+        for k in range(SLOTS * BLK // CHUNK):
+            forward(k)
+
+        @pl.when(t >= 3)
         def _():
-            send_first(t - 1)
-
-        @pl.when(t >= 2)
-        def _():
-            send_second(t - 2)
+            send_second(t - 3)
 
         raw = logit[...]
         ok = valid[...] > 0.5
@@ -350,28 +345,23 @@
         seen = jnp.sum(jnp.where(hit, raw, 0.0), axis=0)
         losses[t] = top + jnp.log(total) - seen
 
-        def backward(k, carry):
-            rows = pl.ds(pl.multiple_of(k * ROWS, ROWS), ROWS)
-            gl = grad_logit[pl.ds(k * BLK, BLK)].reshape(ROWS, LANES)
+        for k in range(REACH):
+            rows = slice(k * ROWS, (k + 1) * ROWS)
+            gl = grad_logit[k * BLK : (k + 1) * BLK].reshape(ROWS, LANES)
             wide = jnp.concatenate([gl] * (HIDDEN // LANES), axis=1)
             grad_hid[t, rows] = ((wide * out_rows[t, 0:1]) * slope[rows]).astype(BF16)
-            return carry
-
-        lax.fori_loop(0, REACH, backward, 0)
 
         weight_grad(t)
         to_core(t).start()
 
-        @pl.when(t >= 2)
+        @pl.when(t >= 1)
         def _():
-            send_z(t - 2)
+            send_first(t - 1)
 
         return carry
 
     lax.fori_loop(0, tissues, tissue, 0)
     last = tissues - 1
-    send_second(last - 1)
-
     def after(low, high):
         rows = slice(low * ROWS, high * ROWS)
         total = None
@@ -383,17 +373,23 @@
                 preferred_element_type=F32,
             )
             total = term if total is None else total + term
-        grad_pre = (total * slope_pre[rows]).reshape((high - low) * BLK, BLK, WIDTH)
+        h = half_pre[rows]
+        u = jnp.tanh(h)
+        steep = 0.5 * ((1.0 + u) * ((1.0 + h) - h * u))
+        grad_pre = (total * steep).reshape((high - low) * BLK, BLK, WIDTH)
         contrib[low:high] = jnp.sum(grad_pre, axis=1).reshape(high - low, BLK, WIDTH)
         for k in range(max(low, 1), high):
             to_ctx(k).start()
 
+    after(3, REACH)
+    send_second(last - 2)
+    send_z(last - 3)
     send_first(last)
-    after(3, REACH)
+    after(0, 3)
+    send_second(last - 1)
+    send_z(last - 2)
+    send_second(last)
     send_z(last - 1)
-    send_second(last)
-    after(0, 3)
-    send_z(last)
     total = contrib[0]
     for k in range(1, REACH):
         to_ctx(k).wait()
@@ -401,6 +397,7 @@
     by_tis[tis] = total
     for j in range(1, n_tis):
         to_tis(j).start()
+    send_z(last)
     wide_eye = lax.broadcasted_iota(jnp.int32, (BLK, LANES), 0) == lane_row
     for t in range(tissues):
         line = jnp.sum(jnp.where(wide_eye, losses[t], 0.0), axis=0, keepdims=True)
@@ -422,6 +419,17 @@
     for j in range(1, n_tis):
         total = total + by_tis[j]
     gacc_ref[0] = total
+
+
+def hand_over(*refs):
+    sems = refs[6]
+    copies = [
+        pltpu.make_async_copy(refs[i], refs[3 + i], sems.at[i]) for i in range(3)
+    ]
+    for copy in copies:
+        copy.start()
+    for copy in copies:
+        copy.wait()
 
 
 def solution(mesh):
@@ -486,7 +494,7 @@
             pltpu.SemaphoreType.DMA((n_tis - 1,)),
             pltpu.SemaphoreType.DMA((n_tis - 1,)),
         ]
-        loss, grad_hidden, grad_acceptor = pl.pallas_call(
+        results = pl.pallas_call(
             functools.partial(kernel, (n_ctx, n_tis, n_rep, tissues)),
             out_shape=(
                 jax.ShapeDtypeStruct((1, tissues, BLK), F32),
@@ -500,6 +508,13 @@
                 collective_id=0, has_side_effects=True, vmem_limit_bytes=60 << 20
             ),
         )(don, acc, dpos, apos, mask, jnp.swapaxes(goal, 1, 2), table, w, wo)
+        loss, grad_hidden, grad_acceptor = pl.pallas_call(
+            hand_over,
+            out_shape=tuple(jax.ShapeDtypeStruct(r.shape, r.dtype) for r in results),
+            in_specs=[vmem] * 3,
+            out_specs=(hbm,) * 3,
+            scratch_shapes=[pltpu.SemaphoreType.DMA((3,))],
+        )(*results)
         return jnp.swapaxes(loss, 1, 2), grad_hidden, grad_acceptor
 
     placed = (

time: 56.2 us -> 45.2 us (0.80)
  Pallas kernels: 52 us -> 44.3 us
  local copies, waits for them, and re-layouts: 3.25 us -> 0 us
    pallas_call x1, Pallas kernels: 52 us -> 42.9 us  [on_device(): pl.pallas_call(functools.partial(kernel, (n_ctx, n_tis, n_rep, tissues)),...]
    unnamed x7 -> x0, local copies, waits for them, and re-layouts: 3.25 us -> none
    pallas_call x0 -> x1, Pallas kernels: none -> 1.41 us  [on_device(): pl.pallas_call(hand_over, out_shape=tuple((jax.ShapeDtypeStruct(r.shape,...]
where the time goes in v3:
time: 45.2 us; the launch traced here: 45 us
  Pallas kernels  44.3 us (98%)
  between operations  0.64 us (1%)
    pallas_call x1, Pallas kernels, on_device(): pl.pallas_call(functools.partial(kernel, (n_ctx, n_tis, n_rep, tissues)),...  42.9 us
    pallas_call x1, Pallas kernels, on_device(): pl.pallas_call(hand_over, out_shape=tuple((jax.ShapeDtypeStruct(r.shape,...  1.41 us

profile of v3, /device:TPU:1, one launch (start us, length us, event | category | flops | bytes accessed | tf_op | source)
XLA Modules:
  0.0 45.0 jit_solution(3109429786128972418)
XLA Ops:
  0.6 42.9 %shard_map.112 = (f32[1,4,16]{2,1,0:T(4,128)}, f32[4,4,512]{2,1,0:T(4,128)}, f32[1,16,256]{2,1,0:T(8,128)}) custom-call(bf16[1,16,256]{2,1,0:T(8,128)(2,1)} %don_in.1, bf16[1,16,256]{2,1,0:T(8,128)(2,1)} %acc_in.1, s32[1,16]{1,0:T(1,128)} %dpos_in.1, s32[1,256]{1,0:T(1,128)} %apos_in.1, s32[1,16,80]{2,1,0:T(8,128)} %mask_in.1, s32[1,4,16]{2,1,0:T(4,128)} %bitcast.2, ...), custom_call_target="tpu_custom_call" | custom-call | tf_op jit(solution)/shard_map/pallas_call | solution.py:497
  43.5 1.4 %shard_map.113 = (f32[1,4,16]{2,1,0:T(4,128)}, f32[4,4,512]{2,1,0:T(4,128)}, f32[1,16,256]{2,1,0:T(8,128)}) custom-call(f32[1,4,16]{2,1,0:T(4,128)} %get-tuple-element.9.refs_0_, f32[4,4,512]{2,1,0:T(4,128)} %get-tuple-element.10.refs_1_, f32[1,16,256]{2,1,0:T(8,128)} %get-tuple-element.11.refs_2_), custom_call_target="tpu_custom_call" | custom-call | tf_op jit(solution)/shard_map/pallas_call | solution.py:511

commit v4 on v3

--- a/solution.py
+++ b/solution.py
@@ -21,7 +21,6 @@
 WIDTH = 256
 HIDDEN = 512
 LANES = 128
-CHUNK = 640
 
 
 def kernel(
@@ -66,6 +65,9 @@
     by_rep,
     from_first,
     from_second,
+    last_own,
+    last_rep,
+    from_rep,
     by_z,
     from_z,
     contrib,
@@ -80,6 +82,8 @@
     first_recv,
     second_send,
     second_recv,
+    rep_send,
+    rep_recv,
     z_send,
     z_recv,
     ctx_send,
@@ -118,7 +122,7 @@
 
     def halo(k):
         return remote(
-            acc_in.at[0], window.at[k], halo_send.at[k - 1], halo_recv.at[k - 1], at_ctx(-k)
+            window.at[0], window.at[k], halo_send.at[k - 1], halo_recv.at[k - 1], at_ctx(-k)
         )
 
     def to_core(t):
@@ -145,6 +149,11 @@
             second_send.at[t, half],
             second_recv.at[t, half],
             {"rep": flip[1 - half]},
+        )
+
+    def to_rep(j):
+        return remote(
+            last_rep.at[j - 1], from_rep.at[j - 1], rep_send.at[j - 1], rep_recv.at[j - 1], at_rep(j)
         )
 
     def to_z(t, j):
@@ -188,8 +197,6 @@
             ]
         )
     ]
-    for copy in staged:
-        copy.start()
 
     barrier = pltpu.get_barrier_semaphore()
     near = set(k % n_ctx for k in range(-SPAN, SPAN + 1)) | set(range(0, n_ctx, 2))
@@ -197,6 +204,8 @@
     peers += [at_tis(j) for j in range(1, n_tis)] + [at_rep(j) for j in range(1, n_rep)]
     for peer in peers:
         pl.semaphore_signal(barrier, inc=1, device_id=peer, device_id_type=MESH)
+    for copy in staged:
+        copy.start()
     for copy in staged[:-1]:
         copy.wait()
     mpad[...] = jnp.zeros_like(mpad)
@@ -238,7 +247,7 @@
     ones = jnp.ones((LANES, LANES), BF16)
     donors = don_ref[0].astype(F32)
 
-    def before(k):
+    def prepare(k, carry):
         base = (ctx + k) * BLK
         dist = jnp.stack(
             [
@@ -253,25 +262,49 @@
         allowed = jnp.dot(
             picked.astype(BF16).reshape(ROWS, LANES), ones, preferred_element_type=F32
         ).reshape(BLK, BLK, LANES)
-        exists = ctx + k < n_ctx
         ok = (allowed > 0.5) & (dist > 0) & (dist <= SPAN * BLOCK_BP)
         ok = jnp.where(ok, 1.0, 0.0)
-        valid[pl.ds(k * BLK, BLK)] = jnp.where(exists, ok, 0.0)
-        feats = jnp.where(exists, window[k].astype(F32), 0.0)
-        pre = table.reshape(BLK, BLK, WIDTH) + donors[None] + feats[:, None, :]
-        h = 0.5 * pre.reshape(ROWS, WIDTH)
+        valid[pl.ds(k * BLK, BLK)] = jnp.where(ctx + k < n_ctx, ok, 0.0)
+        half = 0.5 * (table.reshape(BLK, BLK, WIDTH) + donors[None])
+        half_pre[pl.ds(pl.multiple_of(k * ROWS, ROWS), ROWS)] = half.reshape(ROWS, WIDTH)
+        return carry
+
+    def before(k):
+        rows = pl.ds(pl.multiple_of(k * ROWS, ROWS), ROWS)
+        feats = jnp.where(ctx + k < n_ctx, 0.5 * window[k].astype(F32), 0.0)
+        h = half_pre[rows].reshape(BLK, BLK, WIDTH) + feats[:, None, :]
+        h = h.reshape(ROWS, WIDTH)
+        half_pre[rows] = h
+        u = jnp.tanh(h)
+        pair = 0.5 * (h + h * u).astype(BF16).astype(F32)
+        half = pair.astype(BF16)
+        half_pair[rows] = half
+        pair_t[:, rows] = lax.dot_general(
+            perm[...], half, (((1,), (1,)), ((), ())), preferred_element_type=F32
+        ).astype(BF16)
+
+    def forward(t, low, high):
+        rows = slice(low * BLK, high * BLK)
+        h = jnp.dot(half_pair[rows], w_ref[t], preferred_element_type=F32)
         u = jnp.tanh(h)
         p = h * u
-        pair = 0.5 * (h + p).astype(BF16).astype(F32)
-        half = pair.astype(BF16)
-        half_pair[pl.ds(pl.multiple_of(k * ROWS, ROWS), ROWS)] = half
-        half_pre[pl.ds(pl.multiple_of(k * ROWS, ROWS), ROWS)] = h
-        flipped = lax.dot_general(
-            perm[...], half, (((1,), (1,)), ((), ())), preferred_element_type=F32
-        ).astype(BF16)
-        pair_t[:, pl.ds(pl.multiple_of(k * ROWS, ROWS), ROWS)] = flipped
-
+        slope[t, rows] = (1.0 + u) * ((1.0 + h) - p)
+        logit[t, low:high] = lax.dot_general(
+            (h + p).astype(BF16),
+            out_cols[t],
+            (((1,), (1,)), ((), ())),
+            preferred_element_type=F32,
+        ).reshape(high - low, BLK, LANES)
+
+    lax.fori_loop(0, REACH, prepare, 0)
     before(0)
+    staged[-1].wait()
+
+    def first_block(t, carry):
+        forward(t, 0, BLK)
+        return carry
+
+    lax.fori_loop(0, tissues, first_block, 0)
 
     def more(k, carry):
         halo(k).wait()
@@ -306,36 +339,39 @@
         for j in range(1, n_z):
             to_z(t, j).start()
 
-    def weight_grad(t):
-        total = jnp.dot(pair_t[...], grad_hid[t], preferred_element_type=F32)
-        total = total.reshape(2, per_core, HIDDEN)
-        part[t, :, 0] = total[:, :, :WIDTH]
-        part[t, :, 1] = total[:, :, WIDTH:]
-
-    staged[-1].wait()
+    def send_rep(t):
+        to_core(t).wait()
+        for j in (2, 1, 3, 0):
+            rows = pl.ds(pl.multiple_of(lax.rem(rep + j, n_rep) * per_rep, per_rep), per_rep)
+            for half in range(2):
+                cols = slice(half * WIDTH, (half + 1) * WIDTH)
+                total = part[t, core, half, rows] + from_core[t, half, rows]
+                if j:
+                    last_rep[j - 1, :, cols] = total.astype(BF16)
+                else:
+                    last_own[:, cols] = total
+            if j:
+                to_rep(j).start()
+
+    def send_last_z(t):
+        total = last_own[...]
+        for j in range(1, n_rep):
+            to_rep(j).wait()
+            total = total + from_rep[j - 1].astype(F32)
+        for i in range(n_z):
+            by_z[t, i] = total[i * deep : (i + 1) * deep]
+        for j in range(1, n_z):
+            to_z(t, j).start()
 
     def tissue(t, carry):
-        def forward(k):
-            rows = slice(k * CHUNK, (k + 1) * CHUNK)
-            h = jnp.dot(half_pair[rows], w_ref[t], preferred_element_type=F32)
-            u = jnp.tanh(h)
-            p = h * u
-            slope[rows] = (1.0 + u) * ((1.0 + h) - p)
-            logit[k * (CHUNK // BLK) : (k + 1) * (CHUNK // BLK)] = lax.dot_general(
-                (h + p).astype(BF16),
-                out_cols[t],
-                (((1,), (1,)), ((), ())),
-                preferred_element_type=F32,
-            ).reshape(CHUNK // BLK, BLK, LANES)
-
-        for k in range(SLOTS * BLK // CHUNK):
-            forward(k)
+        forward(t, BLK, 3 * BLK)
+        forward(t, 3 * BLK, SLOTS)
 
         @pl.when(t >= 3)
         def _():
             send_second(t - 3)
 
-        raw = logit[...]
+        raw = logit[t]
         ok = valid[...] > 0.5
         top = jnp.maximum(jnp.max(jnp.where(ok, raw, -jnp.inf), axis=0), 0.0)
         expo = jnp.where(ok, jnp.exp(raw - top[None]), 0.0)
@@ -349,9 +385,11 @@
             rows = slice(k * ROWS, (k + 1) * ROWS)
             gl = grad_logit[k * BLK : (k + 1) * BLK].reshape(ROWS, LANES)
             wide = jnp.concatenate([gl] * (HIDDEN // LANES), axis=1)
-            grad_hid[t, rows] = ((wide * out_rows[t, 0:1]) * slope[rows]).astype(BF16)
-
-        weight_grad(t)
+            grad_hid[t, rows] = ((wide * out_rows[t, 0:1]) * slope[t, rows]).astype(BF16)
+        total = jnp.dot(pair_t[...], grad_hid[t], preferred_element_type=F32)
+        total = total.reshape(2, per_core, HIDDEN)
+        for half in range(2):
+            part[t, :, half] = total[:, :, half * WIDTH : (half + 1) * WIDTH]
         to_core(t).start()
 
         @pl.when(t >= 1)
@@ -384,12 +422,12 @@
     after(3, REACH)
     send_second(last - 2)
     send_z(last - 3)
-    send_first(last)
-    after(0, 3)
+    send_rep(last)
+    after(1, 3)
     send_second(last - 1)
     send_z(last - 2)
-    send_second(last)
-    send_z(last - 1)
+    after(0, 1)
+    send_last_z(last)
     total = contrib[0]
     for k in range(1, REACH):
         to_ctx(k).wait()
@@ -397,7 +435,7 @@
     by_tis[tis] = total
     for j in range(1, n_tis):
         to_tis(j).start()
-    send_z(last)
+    send_z(last - 1)
     wide_eye = lax.broadcasted_iota(jnp.int32, (BLK, LANES), 0) == lane_row
     for t in range(tissues):
         line = jnp.sum(jnp.where(wide_eye, losses[t], 0.0), axis=0, keepdims=True)
@@ -460,8 +498,8 @@
             pltpu.VMEM((WIDTH, pairs), BF16),
             pltpu.VMEM((pairs, WIDTH), F32),
             pltpu.VMEM((SLOTS, BLK, LANES), F32),
-            pltpu.VMEM((pairs, HIDDEN), F32),
-            pltpu.VMEM((SLOTS, BLK, LANES), F32),
+            pltpu.VMEM((tissues, pairs, HIDDEN), F32),
+            pltpu.VMEM((tissues, SLOTS, BLK, LANES), F32),
             pltpu.VMEM((SLOTS, BLK, LANES), F32),
             pltpu.VMEM((tissues, pairs, HIDDEN), BF16),
             pltpu.VMEM((tissues, LANES, HIDDEN), BF16),
@@ -473,6 +511,9 @@
             pltpu.VMEM((tissues, 2, n_rep, per_rep, WIDTH), F32),
             pltpu.VMEM((tissues, 2, 2, per_rep, WIDTH), F32),
             pltpu.VMEM((tissues, 2, per_rep, WIDTH), F32),
+            pltpu.VMEM((per_rep, HIDDEN), F32),
+            pltpu.VMEM((n_rep - 1, per_rep, HIDDEN), BF16),
+            pltpu.VMEM((n_rep - 1, per_rep, HIDDEN), BF16),
             pltpu.VMEM((tissues, n_z, deep, HIDDEN), F32),
             pltpu.VMEM((tissues, n_z - 1, deep, HIDDEN), F32),
             pltpu.VMEM((REACH, BLK, WIDTH), F32),
@@ -487,6 +528,8 @@
             pltpu.SemaphoreType.DMA((tissues, 2)),
             pltpu.SemaphoreType.DMA((tissues, 2)),
             pltpu.SemaphoreType.DMA((tissues, 2)),
+            pltpu.SemaphoreType.DMA((n_rep - 1,)),
+            pltpu.SemaphoreType.DMA((n_rep - 1,)),
             pltpu.SemaphoreType.DMA((tissues, n_z - 1)),
             pltpu.SemaphoreType.DMA((tissues, n_z - 1)),
             pltpu.SemaphoreType.DMA((SPAN,)),

time: 45.2 us -> 44.8 us (level)
  no operation moved by 1% of the time
where the time goes in v4:
time: 44.8 us; the launch traced here: 44.5 us
  Pallas kernels  43.9 us (98%)
  between operations  0.64 us (1%)
    pallas_call x1, Pallas kernels, on_device(): pl.pallas_call(functools.partial(kernel, (n_ctx, n_tis, n_rep, tissues)),...  42.5 us
    pallas_call x1, Pallas kernels, on_device(): pl.pallas_call(hand_over, out_shape=tuple((jax.ShapeDtypeStruct(r.shape,...  1.41 us

profile of v4, /device:TPU:1, one launch (start us, length us, event | category | flops | bytes accessed | tf_op | source)
XLA Modules:
  0.0 44.5 jit_solution(12087735827120508176)
XLA Ops:
  0.6 42.5 %shard_map.112 = (f32[1,4,16]{2,1,0:T(4,128)}, f32[4,4,512]{2,1,0:T(4,128)}, f32[1,16,256]{2,1,0:T(8,128)}) custom-call(bf16[1,16,256]{2,1,0:T(8,128)(2,1)} %don_in.1, bf16[1,16,256]{2,1,0:T(8,128)(2,1)} %acc_in.1, s32[1,16]{1,0:T(1,128)} %dpos_in.1, s32[1,256]{1,0:T(1,128)} %apos_in.1, s32[1,16,80]{2,1,0:T(8,128)} %mask_in.1, s32[1,4,16]{2,1,0:T(4,128)} %bitcast.2, ...), custom_call_target="tpu_custom_call" | custom-call | tf_op jit(solution)/shard_map/pallas_call | solution.py:540
  43.1 1.4 %shard_map.113 = (f32[1,4,16]{2,1,0:T(4,128)}, f32[4,4,512]{2,1,0:T(4,128)}, f32[1,16,256]{2,1,0:T(8,128)}) custom-call(f32[1,4,16]{2,1,0:T(4,128)} %get-tuple-element.9.refs_0_, f32[4,4,512]{2,1,0:T(4,128)} %get-tuple-element.10.refs_1_, f32[1,16,256]{2,1,0:T(8,128)} %get-tuple-element.11.refs_2_), custom_call_target="tpu_custom_call" | custom-call | tf_op jit(solution)/shard_map/pallas_call | solution.py:554

commit v5 on v4

--- a/solution.py
+++ b/solution.py
@@ -62,11 +62,8 @@
     losses,
     part,
     from_core,
+    own_rep,
     by_rep,
-    from_first,
-    from_second,
-    last_own,
-    last_rep,
     from_rep,
     by_z,
     from_z,
@@ -78,10 +75,6 @@
     halo_recv,
     core_send,
     core_recv,
-    first_send,
-    first_recv,
-    second_send,
-    second_recv,
     rep_send,
     rep_recv,
     z_send,
@@ -130,30 +123,13 @@
             part.at[t, 1 - core], from_core.at[t], core_send.at[t], core_recv.at[t], other_core
         )
 
-    flip = (rep + 1 - 2 * lax.rem(rep, 2), n_rep - 1 - rep)
-    far = lax.rem(rep + 2, n_rep)
-
-    def to_first(t, half):
-        return remote(
-            by_rep.at[t, half, pl.ds(2, 2)],
-            from_first.at[t, half],
-            first_send.at[t, half],
-            first_recv.at[t, half],
-            {"rep": flip[half]},
-        )
-
-    def to_second(t, half):
-        return remote(
-            by_rep.at[t, half, 1],
-            from_second.at[t, half],
-            second_send.at[t, half],
-            second_recv.at[t, half],
-            {"rep": flip[1 - half]},
-        )
-
-    def to_rep(j):
-        return remote(
-            last_rep.at[j - 1], from_rep.at[j - 1], rep_send.at[j - 1], rep_recv.at[j - 1], at_rep(j)
+    def to_rep(t, j):
+        return remote(
+            by_rep.at[t, j - 1],
+            from_rep.at[t, j - 1],
+            rep_send.at[t, j - 1],
+            rep_recv.at[t, j - 1],
+            at_rep(j),
         )
 
     def to_z(t, j):
@@ -316,48 +292,22 @@
     slot_all = lax.broadcasted_iota(jnp.int32, (SLOTS, BLK, LANES), 0)
     lane_row = lax.broadcasted_iota(jnp.int32, (BLK, LANES), 1)
 
-    def send_first(t):
-        to_core(t).wait()
-        for half in range(2):
-            for i, q in enumerate((rep, flip[1 - half], flip[half], far)):
-                rows = pl.ds(pl.multiple_of(q * per_rep, per_rep), per_rep)
-                by_rep[t, half, i] = part[t, core, half, rows] + from_core[t, half, rows]
-            to_first(t, half).start()
-
-    def send_second(t):
-        for half in range(2):
-            to_first(t, half).wait()
-            by_rep[t, half, 1] = by_rep[t, half, 1] + from_first[t, half, 1]
-            to_second(t, half).start()
-
-    def send_z(t):
-        for half in range(2):
-            to_second(t, half).wait()
-            total = by_rep[t, half, 0] + from_first[t, half, 0] + from_second[t, half]
-            for i in range(n_z):
-                by_z[t, i, :, half * WIDTH : (half + 1) * WIDTH] = total[i * deep : (i + 1) * deep]
-        for j in range(1, n_z):
-            to_z(t, j).start()
-
     def send_rep(t):
         to_core(t).wait()
         for j in (2, 1, 3, 0):
             rows = pl.ds(pl.multiple_of(lax.rem(rep + j, n_rep) * per_rep, per_rep), per_rep)
-            for half in range(2):
-                cols = slice(half * WIDTH, (half + 1) * WIDTH)
-                total = part[t, core, half, rows] + from_core[t, half, rows]
-                if j:
-                    last_rep[j - 1, :, cols] = total.astype(BF16)
-                else:
-                    last_own[:, cols] = total
+            total = part[t, core, rows] + from_core[t, rows]
             if j:
-                to_rep(j).start()
-
-    def send_last_z(t):
-        total = last_own[...]
+                by_rep[t, j - 1] = total.astype(BF16)
+                to_rep(t, j).start()
+            else:
+                own_rep[t] = total
+
+    def send_z(t):
+        total = own_rep[t]
         for j in range(1, n_rep):
-            to_rep(j).wait()
-            total = total + from_rep[j - 1].astype(F32)
+            to_rep(t, j).wait()
+            total = total + from_rep[t, j - 1].astype(F32)
         for i in range(n_z):
             by_z[t, i] = total[i * deep : (i + 1) * deep]
         for j in range(1, n_z):
@@ -366,10 +316,6 @@
     def tissue(t, carry):
         forward(t, BLK, 3 * BLK)
         forward(t, 3 * BLK, SLOTS)
-
-        @pl.when(t >= 3)
-        def _():
-            send_second(t - 3)
 
         raw = logit[t]
         ok = valid[...] > 0.5
@@ -387,14 +333,12 @@
             wide = jnp.concatenate([gl] * (HIDDEN // LANES), axis=1)
             grad_hid[t, rows] = ((wide * out_rows[t, 0:1]) * slope[t, rows]).astype(BF16)
         total = jnp.dot(pair_t[...], grad_hid[t], preferred_element_type=F32)
-        total = total.reshape(2, per_core, HIDDEN)
-        for half in range(2):
-            part[t, :, half] = total[:, :, half * WIDTH : (half + 1) * WIDTH]
+        part[t] = total.reshape(2, per_core, HIDDEN)
         to_core(t).start()
 
         @pl.when(t >= 1)
         def _():
-            send_first(t - 1)
+            send_rep(t - 1)
 
         return carry
 
@@ -420,14 +364,13 @@
             to_ctx(k).start()
 
     after(3, REACH)
-    send_second(last - 2)
+    send_rep(last)
     send_z(last - 3)
-    send_rep(last)
     after(1, 3)
-    send_second(last - 1)
     send_z(last - 2)
     after(0, 1)
-    send_last_z(last)
+    send_z(last - 1)
+    send_z(last)
     total = contrib[0]
     for k in range(1, REACH):
         to_ctx(k).wait()
@@ -435,7 +378,6 @@
     by_tis[tis] = total
     for j in range(1, n_tis):
         to_tis(j).start()
-    send_z(last - 1)
     wide_eye = lax.broadcasted_iota(jnp.int32, (BLK, LANES), 0) == lane_row
     for t in range(tissues):
         line = jnp.sum(jnp.where(wide_eye, losses[t], 0.0), axis=0, keepdims=True)
@@ -506,14 +448,11 @@
             pltpu.VMEM((tissues, 8, HIDDEN), F32),
             pltpu.VMEM((tissues, BLK, LANES), jnp.int32),
             pltpu.VMEM((tissues, BLK, LANES), F32),
-            pltpu.VMEM((tissues, 2, 2, per_core, WIDTH), F32),
-            pltpu.VMEM((tissues, 2, per_core, WIDTH), F32),
-            pltpu.VMEM((tissues, 2, n_rep, per_rep, WIDTH), F32),
-            pltpu.VMEM((tissues, 2, 2, per_rep, WIDTH), F32),
-            pltpu.VMEM((tissues, 2, per_rep, WIDTH), F32),
-            pltpu.VMEM((per_rep, HIDDEN), F32),
-            pltpu.VMEM((n_rep - 1, per_rep, HIDDEN), BF16),
-            pltpu.VMEM((n_rep - 1, per_rep, HIDDEN), BF16),
+            pltpu.VMEM((tissues, 2, per_core, HIDDEN), F32),
+            pltpu.VMEM((tissues, per_core, HIDDEN), F32),
+            pltpu.VMEM((tissues, per_rep, HIDDEN), F32),
+            pltpu.VMEM((tissues, n_rep - 1, per_rep, HIDDEN), BF16),
+            pltpu.VMEM((tissues, n_rep - 1, per_rep, HIDDEN), BF16),
             pltpu.VMEM((tissues, n_z, deep, HIDDEN), F32),
             pltpu.VMEM((tissues, n_z - 1, deep, HIDDEN), F32),
             pltpu.VMEM((REACH, BLK, WIDTH), F32),
@@ -524,12 +463,8 @@
             pltpu.SemaphoreType.DMA((SPAN,)),
             pltpu.SemaphoreType.DMA((tissues,)),
             pltpu.SemaphoreType.DMA((tissues,)),
-            pltpu.SemaphoreType.DMA((tissues, 2)),
-            pltpu.SemaphoreType.DMA((tissues, 2)),
-            pltpu.SemaphoreType.DMA((tissues, 2)),
-            pltpu.SemaphoreType.DMA((tissues, 2)),
-            pltpu.SemaphoreType.DMA((n_rep - 1,)),
-            pltpu.SemaphoreType.DMA((n_rep - 1,)),
+            pltpu.SemaphoreType.DMA((tissues, n_rep - 1)),
+            pltpu.SemaphoreType.DMA((tissues, n_rep - 1)),
             pltpu.SemaphoreType.DMA((tissues, n_z - 1)),
             pltpu.SemaphoreType.DMA((tissues, n_z - 1)),
             pltpu.SemaphoreType.DMA((SPAN,)),

time: 44.8 us -> 42.3 us (0.944)
  the two profiles are of different devices: /device:TPU:1 before, /device:TPU:3 now
where the time goes in v5:
time: 42.3 us; the launch traced here: 42.1 us
  Pallas kernels  41.5 us (98%)
  between operations  0.64 us (2%)
    pallas_call x1, Pallas kernels, on_device(): pl.pallas_call(functools.partial(kernel, (n_ctx, n_tis, n_rep, tissues)),...  40.1 us
    pallas_call x1, Pallas kernels, on_device(): pl.pallas_call(hand_over, out_shape=tuple((jax.ShapeDtypeStruct(r.shape,...  1.41 us

profile of v5, /device:TPU:3, one launch (start us, length us, event | category | flops | bytes accessed | tf_op | source)
XLA Modules:
  0.0 42.1 jit_solution(17869490562917755659)
XLA Ops:
  0.6 40.1 %shard_map.112 = (f32[1,4,16]{2,1,0:T(4,128)}, f32[4,4,512]{2,1,0:T(4,128)}, f32[1,16,256]{2,1,0:T(8,128)}) custom-call(bf16[1,16,256]{2,1,0:T(8,128)(2,1)} %don_in.1, bf16[1,16,256]{2,1,0:T(8,128)(2,1)} %acc_in.1, s32[1,16]{1,0:T(1,128)} %dpos_in.1, s32[1,256]{1,0:T(1,128)} %apos_in.1, s32[1,16,80]{2,1,0:T(8,128)} %mask_in.1, s32[1,4,16]{2,1,0:T(4,128)} %bitcast.2, ...), custom_call_target="tpu_custom_call" | custom-call | tf_op jit(solution)/shard_map/pallas_call | solution.py:475
  40.7 1.4 %shard_map.113 = (f32[1,4,16]{2,1,0:T(4,128)}, f32[4,4,512]{2,1,0:T(4,128)}, f32[1,16,256]{2,1,0:T(8,128)}) custom-call(f32[1,4,16]{2,1,0:T(4,128)} %get-tuple-element.9.refs_0_, f32[4,4,512]{2,1,0:T(4,128)} %get-tuple-element.10.refs_1_, f32[1,16,256]{2,1,0:T(8,128)} %get-tuple-element.11.refs_2_), custom_call_target="tpu_custom_call" | custom-call | tf_op jit(solution)/shard_map/pallas_call | solution.py:489

commit v6 on v5

--- a/solution.py
+++ b/solution.py
@@ -184,6 +184,12 @@
         copy.start()
     for copy in staged[:-1]:
         copy.wait()
+
+    pl.semaphore_wait(barrier, len(peers))
+
+    for k in reversed(range(1, REACH)):
+        halo(k).start()
+
     mpad[...] = jnp.zeros_like(mpad)
     mpad[:, 0:SLOTS] = mask_ref[0].astype(F32)
     row = lax.broadcasted_iota(jnp.int32, (WIDTH, WIDTH), 0)
@@ -213,17 +219,12 @@
     dcol = column(dpos_ref[...])
     for t in range(tissues):
         goals[t] = column(goal_ref[0, t : t + 1, :])
-    pl.semaphore_wait(barrier, len(peers))
-
-    for k in reversed(range(1, REACH)):
-        halo(k).start()
-
     lane = lax.broadcasted_iota(jnp.int32, (BLK, BLK, LANES), 2)
     slot_in = lax.broadcasted_iota(jnp.int32, (BLK, BLK, LANES), 0)
     ones = jnp.ones((LANES, LANES), BF16)
     donors = don_ref[0].astype(F32)
 
-    def prepare(k, carry):
+    def prepare(k):
         base = (ctx + k) * BLK
         dist = jnp.stack(
             [
@@ -240,13 +241,12 @@
         ).reshape(BLK, BLK, LANES)
         ok = (allowed > 0.5) & (dist > 0) & (dist <= SPAN * BLOCK_BP)
         ok = jnp.where(ok, 1.0, 0.0)
-        valid[pl.ds(k * BLK, BLK)] = jnp.where(ctx + k < n_ctx, ok, 0.0)
+        valid[k * BLK : (k + 1) * BLK] = jnp.where(ctx + k < n_ctx, ok, 0.0)
         half = 0.5 * (table.reshape(BLK, BLK, WIDTH) + donors[None])
-        half_pre[pl.ds(pl.multiple_of(k * ROWS, ROWS), ROWS)] = half.reshape(ROWS, WIDTH)
-        return carry
+        half_pre[k * ROWS : (k + 1) * ROWS] = half.reshape(ROWS, WIDTH)
 
     def before(k):
-        rows = pl.ds(pl.multiple_of(k * ROWS, ROWS), ROWS)
+        rows = slice(k * ROWS, (k + 1) * ROWS)
         feats = jnp.where(ctx + k < n_ctx, 0.5 * window[k].astype(F32), 0.0)
         h = half_pre[rows].reshape(BLK, BLK, WIDTH) + feats[:, None, :]
         h = h.reshape(ROWS, WIDTH)
@@ -272,22 +272,16 @@
             preferred_element_type=F32,
         ).reshape(high - low, BLK, LANES)
 
-    lax.fori_loop(0, REACH, prepare, 0)
+    for k in range(REACH):
+        prepare(k)
     before(0)
     staged[-1].wait()
 
-    def first_block(t, carry):
+    for t in range(tissues):
         forward(t, 0, BLK)
-        return carry
-
-    lax.fori_loop(0, tissues, first_block, 0)
-
-    def more(k, carry):
+    for k in range(1, REACH):
         halo(k).wait()
         before(k)
-        return carry
-
-    lax.fori_loop(1, REACH, more, 0)
 
     slot_all = lax.broadcasted_iota(jnp.int32, (SLOTS, BLK, LANES), 0)
     lane_row = lax.broadcasted_iota(jnp.int32, (BLK, LANES), 1)

time: 42.3 us -> 42.5 us (level)
  the two profiles are of different devices: /device:TPU:3 before, /device:TPU:5 now
where the time goes in v6:
time: 42.5 us; the launch traced here: 42.3 us
  Pallas kernels  41.6 us (98%)
  between operations  0.64 us (2%)
    pallas_call x1, Pallas kernels, on_device(): pl.pallas_call(functools.partial(kernel, (n_ctx, n_tis, n_rep, tissues)),...  40.2 us
    pallas_call x1, Pallas kernels, on_device(): pl.pallas_call(hand_over, out_shape=tuple((jax.ShapeDtypeStruct(r.shape,...  1.41 us

profile of v6, /device:TPU:5, one launch (start us, length us, event | category | flops | bytes accessed | tf_op | source)
XLA Modules:
  0.0 42.3 jit_solution(8521854346126194243)
XLA Ops:
  0.6 40.2 %shard_map.112 = (f32[1,4,16]{2,1,0:T(4,128)}, f32[4,4,512]{2,1,0:T(4,128)}, f32[1,16,256]{2,1,0:T(8,128)}) custom-call(bf16[1,16,256]{2,1,0:T(8,128)(2,1)} %don_in.1, bf16[1,16,256]{2,1,0:T(8,128)(2,1)} %acc_in.1, s32[1,16]{1,0:T(1,128)} %dpos_in.1, s32[1,256]{1,0:T(1,128)} %apos_in.1, s32[1,16,80]{2,1,0:T(8,128)} %mask_in.1, s32[1,4,16]{2,1,0:T(4,128)} %bitcast.2, ...), custom_call_target="tpu_custom_call" | custom-call | tf_op jit(solution)/shard_map/pallas_call | solution.py:469
  40.9 1.4 %shard_map.113 = (f32[1,4,16]{2,1,0:T(4,128)}, f32[4,4,512]{2,1,0:T(4,128)}, f32[1,16,256]{2,1,0:T(8,128)}) custom-call(f32[1,4,16]{2,1,0:T(4,128)} %get-tuple-element.9.refs_0_, f32[4,4,512]{2,1,0:T(4,128)} %get-tuple-element.10.refs_1_, f32[1,16,256]{2,1,0:T(8,128)} %get-tuple-element.11.refs_2_), custom_call_target="tpu_custom_call" | custom-call | tf_op jit(solution)/shard_map/pallas_call | solution.py:483
